TPU v7x, 32 devices: a whole 2x2x4 slice. The times are simulated.
32 devices in a mesh: ax: 4 (over x, core), rad: 8 (over z, y).
Axes of the slice: x: 2, y: 2, z: 4, core: 2. Of those that a mesh axis runs over, the one named last changes fastest.
Arguments:
- sources: float32 [8, 16, 200, 128], P('ax', 'rad'), may hold values from -0.6 to 0.6
- block_inverse: float32 [8, 16, 200, 200], P('ax', 'rad'), may hold values from -2 to 2, as said below
- radial_coupling: float32 [8, 16, 2, 200], P('ax', 'rad'), may hold values from 0.2 to 1.2
- axial_coupling: float32 [8, 16, 4, 200], P('ax', 'rad'), may hold values from 0.01 to 0.05
Outputs:
- correction: float32 [8, 16, 200, 128], P('ax', 'rad')
Inputs may be any that keep to these rules, and one draw needn't show every extreme that they name: `block_inverse`: the given inverse of each cell's diagonal block.
All inputs are finite; a program needn't handle non-finite values.
Results may differ from a plain program's by a relative error of at most 0.00014.
Values sent between devices are 32-bit elements; how exact they have to be, the bound alone decides.
A program may use at most 64 MiB of HBM per device.

v0:
```python
import jax
import jax.numpy as jnp
from jax import lax
from jax.sharding import PartitionSpec as P

SWEEPS = 2


def padded_2(block, sides, width):
    for axis, dim in sides:
        count = lax.axis_size(axis)
        forward = [(i, i + 1) for i in range(count - 1)]
        backward = [(target, source) for source, target in forward]
        low = lax.ppermute(
            lax.slice_in_dim(block, block.shape[dim] - width, None, axis=dim), axis, forward
        )
        high = lax.ppermute(lax.slice_in_dim(block, 0, width, axis=dim), axis, backward)
        block = jnp.concatenate([low, block, high], axis=dim)
    return block


def from_behind(value, axis, steps):
    count = lax.axis_size(axis)
    first, last = (max(0, -steps), min(count, count - steps))
    return lax.ppermute(value, axis, [(source, source + steps) for source in range(first, last)])


def apply_block(inverse_row, operand):
    return jnp.einsum("aij,ajk->aik", inverse_row, operand, precision=lax.Precision.HIGHEST)


def inner_pass(line_source, block_inverse, inward_coupling, incoming):
    values = []
    previous = incoming
    for radial in range(line_source.shape[1]):
        shifted = line_source[:, radial] - inward_coupling[:, radial, :, None] * previous
        previous = apply_block(block_inverse[:, radial], shifted)
        values.append(previous)
    return (jnp.stack(values, 1), previous)


def outer_pass(inner_value, block_inverse, outward_coupling, incoming):
    values = []
    following = incoming
    for radial in reversed(range(inner_value.shape[1])):
        shifted = outward_coupling[:, radial, :, None] * following
        following = inner_value[:, radial] - apply_block(block_inverse[:, radial], shifted)
        values.append(following)
    return (jnp.stack(values[::-1], 1), following)


def chain_matrix(block_inverse, coupling, visiting):
    stations, species = (block_inverse.shape[0], block_inverse.shape[2])
    product = jnp.broadcast_to(jnp.eye(species, dtype=jnp.float32), (stations, species, species))
    for radial in visiting:
        product = -apply_block(block_inverse[:, radial], coupling[:, radial, :, None] * product)
    return product


def on_device(sources, block_inverse, radial_coupling, axial_coupling):
    stations, radial_cells, species, columns = sources.shape
    inward_coupling = radial_coupling[:, :, 0]
    outward_coupling = radial_coupling[:, :, 1]
    zero_field = jnp.zeros((stations, species, columns), jnp.float32)
    inner_matrix = chain_matrix(block_inverse, inward_coupling, list(range(radial_cells)))
    outer_matrix = chain_matrix(
        block_inverse, outward_coupling, list(reversed(range(radial_cells)))
    )
    correction = jnp.zeros(sources.shape, jnp.float32)
    for sweep_index in range(SWEEPS):
        if sweep_index == 0:
            line_source = sources
        else:
            padded = padded_2(correction, (("ax", 0),), 2)
            line_source = sources
            line_source = line_source - axial_coupling[:, :, 0, :, None] * padded[0:stations]
            line_source = line_source - axial_coupling[:, :, 1, :, None] * padded[1 : stations + 1]
            line_source = line_source - axial_coupling[:, :, 2, :, None] * padded[3 : stations + 3]
            line_source = line_source - axial_coupling[:, :, 3, :, None] * padded[4 : stations + 4]
        _, local_last = inner_pass(line_source, block_inverse, inward_coupling, zero_field)

        def pass_inward(section_index, carried):
            outgoing = local_last + apply_block(inner_matrix, carried)
            return from_behind(outgoing, "rad", 1)

        arriving = lax.fori_loop(0, lax.axis_size("rad") - 1, pass_inward, zero_field)
        inner_value, _ = inner_pass(line_source, block_inverse, inward_coupling, arriving)
        _, local_first = outer_pass(inner_value, block_inverse, outward_coupling, zero_field)

        def pass_outward(section_index, carried):
            outgoing = local_first + apply_block(outer_matrix, carried)
            return from_behind(outgoing, "rad", -1)

        arriving = lax.fori_loop(0, lax.axis_size("rad") - 1, pass_outward, zero_field)
        correction, _ = outer_pass(inner_value, block_inverse, outward_coupling, arriving)
    return correction


def solution(mesh):
    placed = (
        P("ax", "rad", None, None),
        P("ax", "rad", None, None),
        P("ax", "rad", None, None),
        P("ax", "rad", None, None),
    )
    return jax.shard_map(
        on_device, mesh=mesh, in_specs=placed, out_specs=P("ax", "rad", None, None), check_vma=False
    )
```

profile of v0, /device:TPU:6, one launch (start us, length us, event | category | flops | bytes accessed | tf_op | source)
XLA Modules:
  0.0 291.9 jit_solution(8426917453913379890)
XLA Ops:
  0.7 2.0 fusion.2
  5.5 63.4 %while.40 = (s32[]{:T(128)}, f32[2,200,128]{2,1,0:T(8,128)S(1)}, f32[2,200,200]{2,1,0:T(8,128)S(1)}, f32[2,200,128]{2,1,0:T(8,128)S(1)}, s32[]{:T(128)}) while((s32[]{:T(128)}, f32[2,200,128]{2,1,0:T(8,128)S(1)}, f32[2,200,200]{2,1,0:T(8,128)S(1)}, f32[2,200,128]{2,1,0:T(8,128)S(1)}, s32[]{:T(128)}) %tuple.74), condition=%wide.region_1.0_spmd, body=%wide.region_0.0_spmd.sunk | while | flops 122931200 | bytes 1753701 | solution.py:86
  6.0 3.4 %collective-permute-start = (f32[2,200,128]{2,1,0:T(8,128)S(1)}, f32[2,200,128]{2,1,0:T(8,128)S(1)}, u32[]{:S(2)}, u32[]{:S(2)}) collective-permute-start(f32[2,200,128]{2,1,0:T(8,128)S(1)} %convolution_add_fusion.8), channel_id=1, source_target_pairs={{0,1},{1,2},{2,3},{3,4},{4,5},{5,6},{6,7},{8,9},{9,10},{10,11},{11... | collective-permute-start | bytes 614408 | tf_op jit(solution)/shard_map/while/body/eval_jaxpr/ppermute | solution.py:25
  9.4 5.3 %collective-permute-done = f32[2,200,128]{2,1,0:T(8,128)S(1)} collective-permute-done((f32[2,200,128]{2,1,0:T(8,128)S(1)}, f32[2,200,128]{2,1,0:T(8,128)S(1)}, u32[]{:S(2)}, u32[]{:S(2)}) %collective-permute-start) | collective-permute-done | bytes 204832 | tf_op jit(solution)/shard_map/while/body/eval_jaxpr/ppermute | solution.py:25
  15.2 4.3 %collective-permute-start = (f32[2,200,128]{2,1,0:T(8,128)S(1)}, f32[2,200,128]{2,1,0:T(8,128)S(1)}, u32[]{:S(2)}, u32[]{:S(2)}) collective-permute-start(f32[2,200,128]{2,1,0:T(8,128)S(1)} %convolution_add_fusion.8), channel_id=1, source_target_pairs={{0,1},{1,2},{2,3},{3,4},{4,5},{5,6},{6,7},{8,9},{9,10},{10,11},{11... | collective-permute-start | bytes 614408 | tf_op jit(solution)/shard_map/while/body/eval_jaxpr/ppermute | solution.py:25
  19.5 3.5 %collective-permute-done = f32[2,200,128]{2,1,0:T(8,128)S(1)} collective-permute-done((f32[2,200,128]{2,1,0:T(8,128)S(1)}, f32[2,200,128]{2,1,0:T(8,128)S(1)}, u32[]{:S(2)}, u32[]{:S(2)}) %collective-permute-start) | collective-permute-done | bytes 204832 | tf_op jit(solution)/shard_map/while/body/eval_jaxpr/ppermute | solution.py:25
  23.6 5.2 %collective-permute-start = (f32[2,200,128]{2,1,0:T(8,128)S(1)}, f32[2,200,128]{2,1,0:T(8,128)S(1)}, u32[]{:S(2)}, u32[]{:S(2)}) collective-permute-start(f32[2,200,128]{2,1,0:T(8,128)S(1)} %convolution_add_fusion.8), channel_id=1, source_target_pairs={{0,1},{1,2},{2,3},{3,4},{4,5},{5,6},{6,7},{8,9},{9,10},{10,11},{11... | collective-permute-start | bytes 614408 | tf_op jit(solution)/shard_map/while/body/eval_jaxpr/ppermute | solution.py:25
  28.8 3.3 %collective-permute-done = f32[2,200,128]{2,1,0:T(8,128)S(1)} collective-permute-done((f32[2,200,128]{2,1,0:T(8,128)S(1)}, f32[2,200,128]{2,1,0:T(8,128)S(1)}, u32[]{:S(2)}, u32[]{:S(2)}) %collective-permute-start) | collective-permute-done | bytes 204832 | tf_op jit(solution)/shard_map/while/body/eval_jaxpr/ppermute | solution.py:25
  32.6 5.3 %collective-permute-start = (f32[2,200,128]{2,1,0:T(8,128)S(1)}, f32[2,200,128]{2,1,0:T(8,128)S(1)}, u32[]{:S(2)}, u32[]{:S(2)}) collective-permute-start(f32[2,200,128]{2,1,0:T(8,128)S(1)} %convolution_add_fusion.8), channel_id=1, source_target_pairs={{0,1},{1,2},{2,3},{3,4},{4,5},{5,6},{6,7},{8,9},{9,10},{10,11},{11... | collective-permute-start | bytes 614408 | tf_op jit(solution)/shard_map/while/body/eval_jaxpr/ppermute | solution.py:25
  37.9 3.3 %collective-permute-done = f32[2,200,128]{2,1,0:T(8,128)S(1)} collective-permute-done((f32[2,200,128]{2,1,0:T(8,128)S(1)}, f32[2,200,128]{2,1,0:T(8,128)S(1)}, u32[]{:S(2)}, u32[]{:S(2)}) %collective-permute-start) | collective-permute-done | bytes 204832 | tf_op jit(solution)/shard_map/while/body/eval_jaxpr/ppermute | solution.py:25
  41.6 5.3 %collective-permute-start = (f32[2,200,128]{2,1,0:T(8,128)S(1)}, f32[2,200,128]{2,1,0:T(8,128)S(1)}, u32[]{:S(2)}, u32[]{:S(2)}) collective-permute-start(f32[2,200,128]{2,1,0:T(8,128)S(1)} %convolution_add_fusion.8), channel_id=1, source_target_pairs={{0,1},{1,2},{2,3},{3,4},{4,5},{5,6},{6,7},{8,9},{9,10},{10,11},{11... | collective-permute-start | bytes 614408 | tf_op jit(solution)/shard_map/while/body/eval_jaxpr/ppermute | solution.py:25
  46.9 3.3 %collective-permute-done = f32[2,200,128]{2,1,0:T(8,128)S(1)} collective-permute-done((f32[2,200,128]{2,1,0:T(8,128)S(1)}, f32[2,200,128]{2,1,0:T(8,128)S(1)}, u32[]{:S(2)}, u32[]{:S(2)}) %collective-permute-start) | collective-permute-done | bytes 204832 | tf_op jit(solution)/shard_map/while/body/eval_jaxpr/ppermute | solution.py:25
  50.7 5.3 %collective-permute-start = (f32[2,200,128]{2,1,0:T(8,128)S(1)}, f32[2,200,128]{2,1,0:T(8,128)S(1)}, u32[]{:S(2)}, u32[]{:S(2)}) collective-permute-start(f32[2,200,128]{2,1,0:T(8,128)S(1)} %convolution_add_fusion.8), channel_id=1, source_target_pairs={{0,1},{1,2},{2,3},{3,4},{4,5},{5,6},{6,7},{8,9},{9,10},{10,11},{11... | collective-permute-start | bytes 614408 | tf_op jit(solution)/shard_map/while/body/eval_jaxpr/ppermute | solution.py:25
  56.0 3.8 %collective-permute-done = f32[2,200,128]{2,1,0:T(8,128)S(1)} collective-permute-done((f32[2,200,128]{2,1,0:T(8,128)S(1)}, f32[2,200,128]{2,1,0:T(8,128)S(1)}, u32[]{:S(2)}, u32[]{:S(2)}) %collective-permute-start) | collective-permute-done | bytes 204832 | tf_op jit(solution)/shard_map/while/body/eval_jaxpr/ppermute | solution.py:25
  60.3 5.3 %collective-permute-start = (f32[2,200,128]{2,1,0:T(8,128)S(1)}, f32[2,200,128]{2,1,0:T(8,128)S(1)}, u32[]{:S(2)}, u32[]{:S(2)}) collective-permute-start(f32[2,200,128]{2,1,0:T(8,128)S(1)} %convolution_add_fusion.8), channel_id=1, source_target_pairs={{0,1},{1,2},{2,3},{3,4},{4,5},{5,6},{6,7},{8,9},{9,10},{10,11},{11... | collective-permute-start | bytes 614408 | tf_op jit(solution)/shard_map/while/body/eval_jaxpr/ppermute | solution.py:25
  65.6 3.3 %collective-permute-done = f32[2,200,128]{2,1,0:T(8,128)S(1)} collective-permute-done((f32[2,200,128]{2,1,0:T(8,128)S(1)}, f32[2,200,128]{2,1,0:T(8,128)S(1)}, u32[]{:S(2)}, u32[]{:S(2)}) %collective-permute-start) | collective-permute-done | bytes 204832 | tf_op jit(solution)/shard_map/while/body/eval_jaxpr/ppermute | solution.py:25
  73.1 66.7 %while.41 = (s32[]{:T(128)}, f32[2,200,128]{2,1,0:T(8,128)S(1)}, f32[2,200,200]{2,1,0:T(8,128)S(1)}, f32[2,200,128]{2,1,0:T(8,128)S(1)}, s32[]{:T(128)}) while((s32[]{:T(128)}, f32[2,200,128]{2,1,0:T(8,128)S(1)}, f32[2,200,200]{2,1,0:T(8,128)S(1)}, f32[2,200,128]{2,1,0:T(8,128)S(1)}, s32[]{:T(128)}) %tuple.77), condition=%wide.region_3.0_spmd, body=%wide.region_2.0_spmd.sunk | while | flops 122931200 | bytes 1753701 | solution.py:94
  73.6 1.9 collective-permute-start.1
  75.6 8.9 %collective-permute-done.1 = f32[2,200,128]{2,1,0:T(8,128)S(1)} collective-permute-done((f32[2,200,128]{2,1,0:T(8,128)S(1)}, f32[2,200,128]{2,1,0:T(8,128)S(1)}, u32[]{:S(2)}, u32[]{:S(2)}) %collective-permute-start.1) | collective-permute-done | bytes 204832 | tf_op jit(solution)/shard_map/while/body/eval_jaxpr/ppermute | solution.py:25
  84.9 1.9 collective-permute-start.1
  86.9 7.6 %collective-permute-done.1 = f32[2,200,128]{2,1,0:T(8,128)S(1)} collective-permute-done((f32[2,200,128]{2,1,0:T(8,128)S(1)}, f32[2,200,128]{2,1,0:T(8,128)S(1)}, u32[]{:S(2)}, u32[]{:S(2)}) %collective-permute-start.1) | collective-permute-done | bytes 204832 | tf_op jit(solution)/shard_map/while/body/eval_jaxpr/ppermute | solution.py:25
  94.9 1.9 collective-permute-start.1
  96.9 6.7 %collective-permute-done.1 = f32[2,200,128]{2,1,0:T(8,128)S(1)} collective-permute-done((f32[2,200,128]{2,1,0:T(8,128)S(1)}, f32[2,200,128]{2,1,0:T(8,128)S(1)}, u32[]{:S(2)}, u32[]{:S(2)}) %collective-permute-start.1) | collective-permute-done | bytes 204832 | tf_op jit(solution)/shard_map/while/body/eval_jaxpr/ppermute | solution.py:25
  104.1 1.9 collective-permute-start.1
  106.0 6.6 %collective-permute-done.1 = f32[2,200,128]{2,1,0:T(8,128)S(1)} collective-permute-done((f32[2,200,128]{2,1,0:T(8,128)S(1)}, f32[2,200,128]{2,1,0:T(8,128)S(1)}, u32[]{:S(2)}, u32[]{:S(2)}) %collective-permute-start.1) | collective-permute-done | bytes 204832 | tf_op jit(solution)/shard_map/while/body/eval_jaxpr/ppermute | solution.py:25
  113.2 1.9 collective-permute-start.1
  115.1 6.6 %collective-permute-done.1 = f32[2,200,128]{2,1,0:T(8,128)S(1)} collective-permute-done((f32[2,200,128]{2,1,0:T(8,128)S(1)}, f32[2,200,128]{2,1,0:T(8,128)S(1)}, u32[]{:S(2)}, u32[]{:S(2)}) %collective-permute-start.1) | collective-permute-done | bytes 204832 | tf_op jit(solution)/shard_map/while/body/eval_jaxpr/ppermute | solution.py:25
  122.2 1.9 collective-permute-start.1
  124.1 6.6 %collective-permute-done.1 = f32[2,200,128]{2,1,0:T(8,128)S(1)} collective-permute-done((f32[2,200,128]{2,1,0:T(8,128)S(1)}, f32[2,200,128]{2,1,0:T(8,128)S(1)}, u32[]{:S(2)}, u32[]{:S(2)}) %collective-permute-start.1) | collective-permute-done | bytes 204832 | tf_op jit(solution)/shard_map/while/body/eval_jaxpr/ppermute | solution.py:25
  131.3 1.9 collective-permute-start.1
  133.2 6.6 %collective-permute-done.1 = f32[2,200,128]{2,1,0:T(8,128)S(1)} collective-permute-done((f32[2,200,128]{2,1,0:T(8,128)S(1)}, f32[2,200,128]{2,1,0:T(8,128)S(1)}, u32[]{:S(2)}, u32[]{:S(2)}) %collective-permute-start.1) | collective-permute-done | bytes 204832 | tf_op jit(solution)/shard_map/while/body/eval_jaxpr/ppermute | solution.py:25
  141.1 1.9 collective-permute-start.4
  143.0 3.8 %collective-permute-start.5 = (f32[2,2,200,128]{3,2,0,1:T(8,128)S(1)}, f32[2,2,200,128]{3,2,0,1:T(8,128)}, u32[]{:S(2)}, u32[]{:S(2)}) collective-permute-start(f32[2,2,200,128]{3,2,0,1:T(8,128)S(1)} %pad_maximum_fusion.4), channel_id=1, source_target_pairs={{8,0},{16,8},{24,16},{9,1},{17,9},{25,17},{10,2},{18,10},{26,18},{... | collective-permute-start | bytes 1228808 | tf_op jit(solution)/shard_map/ppermute | solution.py:17
  146.9 3.5 %collective-permute-done.4 = f32[2,2,200,128]{3,2,0,1:T(8,128)S(1)} collective-permute-done((f32[2,2,200,128]{3,2,0,1:T(8,128)S(1)}, f32[2,2,200,128]{3,2,0,1:T(8,128)S(1)}, u32[]{:S(2)}, u32[]{:S(2)}) %collective-permute-start.4) | collective-permute-done | bytes 409632 | tf_op jit(solution)/shard_map/ppermute | solution.py:14
  154.8 64.9 %while.42 = (s32[]{:T(128)}, f32[2,200,128]{2,1,0:T(8,128)S(1)}, f32[2,200,200]{2,1,0:T(8,128)S(1)}, f32[2,200,128]{2,1,0:T(8,128)S(1)}, s32[]{:T(128)}) while((s32[]{:T(128)}, f32[2,200,128]{2,1,0:T(8,128)S(1)}, f32[2,200,200]{2,1,0:T(8,128)S(1)}, f32[2,200,128]{2,1,0:T(8,128)S(1)}, s32[]{:T(128)}) %tuple.86), condition=%wide.region_5.0_spmd, body=%wide.region_4.0_spmd.sunk | while | flops 122931200 | bytes 1753701 | solution.py:86
  155.3 2.0 collective-permute-start.2
  157.4 7.0 %collective-permute-done.2 = f32[2,200,128]{2,1,0:T(8,128)S(1)} collective-permute-done((f32[2,200,128]{2,1,0:T(8,128)S(1)}, f32[2,200,128]{2,1,0:T(8,128)S(1)}, u32[]{:S(2)}, u32[]{:S(2)}) %collective-permute-start.2) | collective-permute-done | bytes 204832 | tf_op jit(solution)/shard_map/while/body/eval_jaxpr/ppermute | solution.py:25
  164.8 2.4 collective-permute-start.2
  167.3 7.1 %collective-permute-done.2 = f32[2,200,128]{2,1,0:T(8,128)S(1)} collective-permute-done((f32[2,200,128]{2,1,0:T(8,128)S(1)}, f32[2,200,128]{2,1,0:T(8,128)S(1)}, u32[]{:S(2)}, u32[]{:S(2)}) %collective-permute-start.2) | collective-permute-done | bytes 204832 | tf_op jit(solution)/shard_map/while/body/eval_jaxpr/ppermute | solution.py:25
  174.9 3.5 %collective-permute-start.2 = (f32[2,200,128]{2,1,0:T(8,128)S(1)}, f32[2,200,128]{2,1,0:T(8,128)S(1)}, u32[]{:S(2)}, u32[]{:S(2)}) collective-permute-start(f32[2,200,128]{2,1,0:T(8,128)S(1)} %convolution_add_fusion.10), channel_id=1, source_target_pairs={{0,1},{1,2},{2,3},{3,4},{4,5},{5,6},{6,7},{8,9},{9,10},{10,11},{11... | collective-permute-start | bytes 614408 | tf_op jit(solution)/shard_map/while/body/eval_jaxpr/ppermute | solution.py:25
  178.4 5.2 %collective-permute-done.2 = f32[2,200,128]{2,1,0:T(8,128)S(1)} collective-permute-done((f32[2,200,128]{2,1,0:T(8,128)S(1)}, f32[2,200,128]{2,1,0:T(8,128)S(1)}, u32[]{:S(2)}, u32[]{:S(2)}) %collective-permute-start.2) | collective-permute-done | bytes 204832 | tf_op jit(solution)/shard_map/while/body/eval_jaxpr/ppermute | solution.py:25
  184.1 4.7 %collective-permute-start.2 = (f32[2,200,128]{2,1,0:T(8,128)S(1)}, f32[2,200,128]{2,1,0:T(8,128)S(1)}, u32[]{:S(2)}, u32[]{:S(2)}) collective-permute-start(f32[2,200,128]{2,1,0:T(8,128)S(1)} %convolution_add_fusion.10), channel_id=1, source_target_pairs={{0,1},{1,2},{2,3},{3,4},{4,5},{5,6},{6,7},{8,9},{9,10},{10,11},{11... | collective-permute-start | bytes 614408 | tf_op jit(solution)/shard_map/while/body/eval_jaxpr/ppermute | solution.py:25
  188.8 3.7 %collective-permute-done.2 = f32[2,200,128]{2,1,0:T(8,128)S(1)} collective-permute-done((f32[2,200,128]{2,1,0:T(8,128)S(1)}, f32[2,200,128]{2,1,0:T(8,128)S(1)}, u32[]{:S(2)}, u32[]{:S(2)}) %collective-permute-start.2) | collective-permute-done | bytes 204832 | tf_op jit(solution)/shard_map/while/body/eval_jaxpr/ppermute | solution.py:25
  193.0 5.3 %collective-permute-start.2 = (f32[2,200,128]{2,1,0:T(8,128)S(1)}, f32[2,200,128]{2,1,0:T(8,128)S(1)}, u32[]{:S(2)}, u32[]{:S(2)}) collective-permute-start(f32[2,200,128]{2,1,0:T(8,128)S(1)} %convolution_add_fusion.10), channel_id=1, source_target_pairs={{0,1},{1,2},{2,3},{3,4},{4,5},{5,6},{6,7},{8,9},{9,10},{10,11},{11... | collective-permute-start | bytes 614408 | tf_op jit(solution)/shard_map/while/body/eval_jaxpr/ppermute | solution.py:25
  198.3 3.3 %collective-permute-done.2 = f32[2,200,128]{2,1,0:T(8,128)S(1)} collective-permute-done((f32[2,200,128]{2,1,0:T(8,128)S(1)}, f32[2,200,128]{2,1,0:T(8,128)S(1)}, u32[]{:S(2)}, u32[]{:S(2)}) %collective-permute-start.2) | collective-permute-done | bytes 204832 | tf_op jit(solution)/shard_map/while/body/eval_jaxpr/ppermute | solution.py:25
  202.1 5.3 %collective-permute-start.2 = (f32[2,200,128]{2,1,0:T(8,128)S(1)}, f32[2,200,128]{2,1,0:T(8,128)S(1)}, u32[]{:S(2)}, u32[]{:S(2)}) collective-permute-start(f32[2,200,128]{2,1,0:T(8,128)S(1)} %convolution_add_fusion.10), channel_id=1, source_target_pairs={{0,1},{1,2},{2,3},{3,4},{4,5},{5,6},{6,7},{8,9},{9,10},{10,11},{11... | collective-permute-start | bytes 614408 | tf_op jit(solution)/shard_map/while/body/eval_jaxpr/ppermute | solution.py:25
  207.4 3.3 %collective-permute-done.2 = f32[2,200,128]{2,1,0:T(8,128)S(1)} collective-permute-done((f32[2,200,128]{2,1,0:T(8,128)S(1)}, f32[2,200,128]{2,1,0:T(8,128)S(1)}, u32[]{:S(2)}, u32[]{:S(2)}) %collective-permute-start.2) | collective-permute-done | bytes 204832 | tf_op jit(solution)/shard_map/while/body/eval_jaxpr/ppermute | solution.py:25
  211.1 5.3 %collective-permute-start.2 = (f32[2,200,128]{2,1,0:T(8,128)S(1)}, f32[2,200,128]{2,1,0:T(8,128)S(1)}, u32[]{:S(2)}, u32[]{:S(2)}) collective-permute-start(f32[2,200,128]{2,1,0:T(8,128)S(1)} %convolution_add_fusion.10), channel_id=1, source_target_pairs={{0,1},{1,2},{2,3},{3,4},{4,5},{5,6},{6,7},{8,9},{9,10},{10,11},{11... | collective-permute-start | bytes 614408 | tf_op jit(solution)/shard_map/while/body/eval_jaxpr/ppermute | solution.py:25
  216.4 3.3 %collective-permute-done.2 = f32[2,200,128]{2,1,0:T(8,128)S(1)} collective-permute-done((f32[2,200,128]{2,1,0:T(8,128)S(1)}, f32[2,200,128]{2,1,0:T(8,128)S(1)}, u32[]{:S(2)}, u32[]{:S(2)}) %collective-permute-start.2) | collective-permute-done | bytes 204832 | tf_op jit(solution)/shard_map/while/body/eval_jaxpr/ppermute | solution.py:25
  221.5 68.4 %while.43 = (s32[]{:T(128)}, f32[2,200,128]{2,1,0:T(8,128)S(1)}, f32[2,200,200]{2,1,0:T(8,128)S(1)}, f32[2,200,128]{2,1,0:T(8,128)S(1)}, s32[]{:T(128)}) while((s32[]{:T(128)}, f32[2,200,128]{2,1,0:T(8,128)S(1)}, f32[2,200,200]{2,1,0:T(8,128)S(1)}, f32[2,200,128]{2,1,0:T(8,128)S(1)}, s32[]{:T(128)}) %tuple.87), condition=%wide.region_7.0_spmd, body=%wide.region_6.0_spmd.sunk | while | flops 122931200 | bytes 1753701 | solution.py:94
  222.0 1.9 collective-permute-start.3
  224.0 7.1 %collective-permute-done.3 = f32[2,200,128]{2,1,0:T(8,128)S(1)} collective-permute-done((f32[2,200,128]{2,1,0:T(8,128)S(1)}, f32[2,200,128]{2,1,0:T(8,128)S(1)}, u32[]{:S(2)}, u32[]{:S(2)}) %collective-permute-start.3) | collective-permute-done | bytes 204832 | tf_op jit(solution)/shard_map/while/body/eval_jaxpr/ppermute | solution.py:25
  231.6 1.9 collective-permute-start.3
  233.5 9.1 %collective-permute-done.3 = f32[2,200,128]{2,1,0:T(8,128)S(1)} collective-permute-done((f32[2,200,128]{2,1,0:T(8,128)S(1)}, f32[2,200,128]{2,1,0:T(8,128)S(1)}, u32[]{:S(2)}, u32[]{:S(2)}) %collective-permute-start.3) | collective-permute-done | bytes 204832 | tf_op jit(solution)/shard_map/while/body/eval_jaxpr/ppermute | solution.py:25
  243.1 1.9 collective-permute-start.3
  245.0 8.1 %collective-permute-done.3 = f32[2,200,128]{2,1,0:T(8,128)S(1)} collective-permute-done((f32[2,200,128]{2,1,0:T(8,128)S(1)}, f32[2,200,128]{2,1,0:T(8,128)S(1)}, u32[]{:S(2)}, u32[]{:S(2)}) %collective-permute-start.3) | collective-permute-done | bytes 204832 | tf_op jit(solution)/shard_map/while/body/eval_jaxpr/ppermute | solution.py:25
  253.6 1.9 collective-permute-start.3
  255.5 7.2 %collective-permute-done.3 = f32[2,200,128]{2,1,0:T(8,128)S(1)} collective-permute-done((f32[2,200,128]{2,1,0:T(8,128)S(1)}, f32[2,200,128]{2,1,0:T(8,128)S(1)}, u32[]{:S(2)}, u32[]{:S(2)}) %collective-permute-start.3) | collective-permute-done | bytes 204832 | tf_op jit(solution)/shard_map/while/body/eval_jaxpr/ppermute | solution.py:25
  263.3 1.9 collective-permute-start.3
  265.2 6.6 %collective-permute-done.3 = f32[2,200,128]{2,1,0:T(8,128)S(1)} collective-permute-done((f32[2,200,128]{2,1,0:T(8,128)S(1)}, f32[2,200,128]{2,1,0:T(8,128)S(1)}, u32[]{:S(2)}, u32[]{:S(2)}) %collective-permute-start.3) | collective-permute-done | bytes 204832 | tf_op jit(solution)/shard_map/while/body/eval_jaxpr/ppermute | solution.py:25
  272.3 1.9 collective-permute-start.3
  274.3 6.6 %collective-permute-done.3 = f32[2,200,128]{2,1,0:T(8,128)S(1)} collective-permute-done((f32[2,200,128]{2,1,0:T(8,128)S(1)}, f32[2,200,128]{2,1,0:T(8,128)S(1)}, u32[]{:S(2)}, u32[]{:S(2)}) %collective-permute-start.3) | collective-permute-done | bytes 204832 | tf_op jit(solution)/shard_map/while/body/eval_jaxpr/ppermute | solution.py:25
  281.4 1.9 collective-permute-start.3
  283.3 6.6 %collective-permute-done.3 = f32[2,200,128]{2,1,0:T(8,128)S(1)} collective-permute-done((f32[2,200,128]{2,1,0:T(8,128)S(1)}, f32[2,200,128]{2,1,0:T(8,128)S(1)}, u32[]{:S(2)}, u32[]{:S(2)}) %collective-permute-start.3) | collective-permute-done | bytes 204832 | tf_op jit(solution)/shard_map/while/body/eval_jaxpr/ppermute | solution.py:25
  (77 shorter events, 31.0 us)
Async XLA Ops:
  0.0 0.7 copy-start.3
  0.0 2.8 copy-start
  3.3 1.0 copy-start.1
  6.0 8.7 %collective-permute-start = (f32[2,200,128]{2,1,0:T(8,128)S(1)}, f32[2,200,128]{2,1,0:T(8,128)S(1)}, u32[]{:S(2)}, u32[]{:S(2)}) collective-permute-start(f32[2,200,128]{2,1,0:T(8,128)S(1)} %convolution_add_fusion.8), channel_id=1, source_target_pairs={{0,1},{1,2},{2,3},{3,4},{4,5},{5,6},{6,7},{8,9},{9,10},{10,11},{11... | collective-permute-start | bytes 614408 | tf_op jit(solution)/shard_map/while/body/eval_jaxpr/ppermute | solution.py:25
  15.2 7.9 %collective-permute-start = (f32[2,200,128]{2,1,0:T(8,128)S(1)}, f32[2,200,128]{2,1,0:T(8,128)S(1)}, u32[]{:S(2)}, u32[]{:S(2)}) collective-permute-start(f32[2,200,128]{2,1,0:T(8,128)S(1)} %convolution_add_fusion.8), channel_id=1, source_target_pairs={{0,1},{1,2},{2,3},{3,4},{4,5},{5,6},{6,7},{8,9},{9,10},{10,11},{11... | collective-permute-start | bytes 614408 | tf_op jit(solution)/shard_map/while/body/eval_jaxpr/ppermute | solution.py:25
  23.6 8.5 %collective-permute-start = (f32[2,200,128]{2,1,0:T(8,128)S(1)}, f32[2,200,128]{2,1,0:T(8,128)S(1)}, u32[]{:S(2)}, u32[]{:S(2)}) collective-permute-start(f32[2,200,128]{2,1,0:T(8,128)S(1)} %convolution_add_fusion.8), channel_id=1, source_target_pairs={{0,1},{1,2},{2,3},{3,4},{4,5},{5,6},{6,7},{8,9},{9,10},{10,11},{11... | collective-permute-start | bytes 614408 | tf_op jit(solution)/shard_map/while/body/eval_jaxpr/ppermute | solution.py:25
  32.6 8.6 %collective-permute-start = (f32[2,200,128]{2,1,0:T(8,128)S(1)}, f32[2,200,128]{2,1,0:T(8,128)S(1)}, u32[]{:S(2)}, u32[]{:S(2)}) collective-permute-start(f32[2,200,128]{2,1,0:T(8,128)S(1)} %convolution_add_fusion.8), channel_id=1, source_target_pairs={{0,1},{1,2},{2,3},{3,4},{4,5},{5,6},{6,7},{8,9},{9,10},{10,11},{11... | collective-permute-start | bytes 614408 | tf_op jit(solution)/shard_map/while/body/eval_jaxpr/ppermute | solution.py:25
  41.6 8.6 %collective-permute-start = (f32[2,200,128]{2,1,0:T(8,128)S(1)}, f32[2,200,128]{2,1,0:T(8,128)S(1)}, u32[]{:S(2)}, u32[]{:S(2)}) collective-permute-start(f32[2,200,128]{2,1,0:T(8,128)S(1)} %convolution_add_fusion.8), channel_id=1, source_target_pairs={{0,1},{1,2},{2,3},{3,4},{4,5},{5,6},{6,7},{8,9},{9,10},{10,11},{11... | collective-permute-start | bytes 614408 | tf_op jit(solution)/shard_map/while/body/eval_jaxpr/ppermute | solution.py:25
  50.7 9.1 %collective-permute-start = (f32[2,200,128]{2,1,0:T(8,128)S(1)}, f32[2,200,128]{2,1,0:T(8,128)S(1)}, u32[]{:S(2)}, u32[]{:S(2)}) collective-permute-start(f32[2,200,128]{2,1,0:T(8,128)S(1)} %convolution_add_fusion.8), channel_id=1, source_target_pairs={{0,1},{1,2},{2,3},{3,4},{4,5},{5,6},{6,7},{8,9},{9,10},{10,11},{11... | collective-permute-start | bytes 614408 | tf_op jit(solution)/shard_map/while/body/eval_jaxpr/ppermute | solution.py:25
  60.3 8.6 %collective-permute-start = (f32[2,200,128]{2,1,0:T(8,128)S(1)}, f32[2,200,128]{2,1,0:T(8,128)S(1)}, u32[]{:S(2)}, u32[]{:S(2)}) collective-permute-start(f32[2,200,128]{2,1,0:T(8,128)S(1)} %convolution_add_fusion.8), channel_id=1, source_target_pairs={{0,1},{1,2},{2,3},{3,4},{4,5},{5,6},{6,7},{8,9},{9,10},{10,11},{11... | collective-permute-start | bytes 614408 | tf_op jit(solution)/shard_map/while/body/eval_jaxpr/ppermute | solution.py:25
  73.6 10.8 %collective-permute-start.1 = (f32[2,200,128]{2,1,0:T(8,128)S(1)}, f32[2,200,128]{2,1,0:T(8,128)S(1)}, u32[]{:S(2)}, u32[]{:S(2)}) collective-permute-start(f32[2,200,128]{2,1,0:T(8,128)S(1)} %convolution_add_fusion.9), channel_id=1, source_target_pairs={{1,0},{2,1},{3,2},{4,3},{5,4},{6,5},{7,6},{9,8},{10,9},{11,10},{12... | collective-permute-start | bytes 614408 | tf_op jit(solution)/shard_map/while/body/eval_jaxpr/ppermute | solution.py:25
  84.9 9.5 %collective-permute-start.1 = (f32[2,200,128]{2,1,0:T(8,128)S(1)}, f32[2,200,128]{2,1,0:T(8,128)S(1)}, u32[]{:S(2)}, u32[]{:S(2)}) collective-permute-start(f32[2,200,128]{2,1,0:T(8,128)S(1)} %convolution_add_fusion.9), channel_id=1, source_target_pairs={{1,0},{2,1},{3,2},{4,3},{5,4},{6,5},{7,6},{9,8},{10,9},{11,10},{12... | collective-permute-start | bytes 614408 | tf_op jit(solution)/shard_map/while/body/eval_jaxpr/ppermute | solution.py:25
  94.9 8.6 %collective-permute-start.1 = (f32[2,200,128]{2,1,0:T(8,128)S(1)}, f32[2,200,128]{2,1,0:T(8,128)S(1)}, u32[]{:S(2)}, u32[]{:S(2)}) collective-permute-start(f32[2,200,128]{2,1,0:T(8,128)S(1)} %convolution_add_fusion.9), channel_id=1, source_target_pairs={{1,0},{2,1},{3,2},{4,3},{5,4},{6,5},{7,6},{9,8},{10,9},{11,10},{12... | collective-permute-start | bytes 614408 | tf_op jit(solution)/shard_map/while/body/eval_jaxpr/ppermute | solution.py:25
  104.1 8.6 %collective-permute-start.1 = (f32[2,200,128]{2,1,0:T(8,128)S(1)}, f32[2,200,128]{2,1,0:T(8,128)S(1)}, u32[]{:S(2)}, u32[]{:S(2)}) collective-permute-start(f32[2,200,128]{2,1,0:T(8,128)S(1)} %convolution_add_fusion.9), channel_id=1, source_target_pairs={{1,0},{2,1},{3,2},{4,3},{5,4},{6,5},{7,6},{9,8},{10,9},{11,10},{12... | collective-permute-start | bytes 614408 | tf_op jit(solution)/shard_map/while/body/eval_jaxpr/ppermute | solution.py:25
  113.2 8.6 %collective-permute-start.1 = (f32[2,200,128]{2,1,0:T(8,128)S(1)}, f32[2,200,128]{2,1,0:T(8,128)S(1)}, u32[]{:S(2)}, u32[]{:S(2)}) collective-permute-start(f32[2,200,128]{2,1,0:T(8,128)S(1)} %convolution_add_fusion.9), channel_id=1, source_target_pairs={{1,0},{2,1},{3,2},{4,3},{5,4},{6,5},{7,6},{9,8},{10,9},{11,10},{12... | collective-permute-start | bytes 614408 | tf_op jit(solution)/shard_map/while/body/eval_jaxpr/ppermute | solution.py:25
  122.2 8.6 %collective-permute-start.1 = (f32[2,200,128]{2,1,0:T(8,128)S(1)}, f32[2,200,128]{2,1,0:T(8,128)S(1)}, u32[]{:S(2)}, u32[]{:S(2)}) collective-permute-start(f32[2,200,128]{2,1,0:T(8,128)S(1)} %convolution_add_fusion.9), channel_id=1, source_target_pairs={{1,0},{2,1},{3,2},{4,3},{5,4},{6,5},{7,6},{9,8},{10,9},{11,10},{12... | collective-permute-start | bytes 614408 | tf_op jit(solution)/shard_map/while/body/eval_jaxpr/ppermute | solution.py:25
  131.3 8.6 %collective-permute-start.1 = (f32[2,200,128]{2,1,0:T(8,128)S(1)}, f32[2,200,128]{2,1,0:T(8,128)S(1)}, u32[]{:S(2)}, u32[]{:S(2)}) collective-permute-start(f32[2,200,128]{2,1,0:T(8,128)S(1)} %convolution_add_fusion.9), channel_id=1, source_target_pairs={{1,0},{2,1},{3,2},{4,3},{5,4},{6,5},{7,6},{9,8},{10,9},{11,10},{12... | collective-permute-start | bytes 614408 | tf_op jit(solution)/shard_map/while/body/eval_jaxpr/ppermute | solution.py:25
  141.0 5.8 %copy-start.2 = (f32[2,2,4,200]{3,2,1,0:T(4,128)S(1)}, f32[2,2,4,200]{3,2,1,0:T(4,128)}, u32[]{:S(2)}) copy-start(f32[2,2,4,200]{3,2,1,0:T(4,128)} %param.15) | copy-start | bytes 38404
  141.1 9.3 %collective-permute-start.4 = (f32[2,2,200,128]{3,2,0,1:T(8,128)S(1)}, f32[2,2,200,128]{3,2,0,1:T(8,128)S(1)}, u32[]{:S(2)}, u32[]{:S(2)}) collective-permute-start(f32[2,2,200,128]{3,2,0,1:T(8,128)S(1)} %pad_maximum_fusion.4), channel_id=1, source_target_pairs={{0,8},{8,16},{16,24},{1,9},{9,17},{17,25},{2,10},{10,18},{18,26},{... | collective-permute-start | bytes 1228808 | tf_op jit(solution)/shard_map/ppermute | solution.py:14
  143.0 9.1 %collective-permute-start.5 = (f32[2,2,200,128]{3,2,0,1:T(8,128)S(1)}, f32[2,2,200,128]{3,2,0,1:T(8,128)}, u32[]{:S(2)}, u32[]{:S(2)}) collective-permute-start(f32[2,2,200,128]{3,2,0,1:T(8,128)S(1)} %pad_maximum_fusion.4), channel_id=1, source_target_pairs={{8,0},{16,8},{24,16},{9,1},{17,9},{25,17},{10,2},{18,10},{26,18},{... | collective-permute-start | bytes 1228808 | tf_op jit(solution)/shard_map/ppermute | solution.py:17
  155.3 9.0 %collective-permute-start.2 = (f32[2,200,128]{2,1,0:T(8,128)S(1)}, f32[2,200,128]{2,1,0:T(8,128)S(1)}, u32[]{:S(2)}, u32[]{:S(2)}) collective-permute-start(f32[2,200,128]{2,1,0:T(8,128)S(1)} %convolution_add_fusion.10), channel_id=1, source_target_pairs={{0,1},{1,2},{2,3},{3,4},{4,5},{5,6},{6,7},{8,9},{9,10},{10,11},{11... | collective-permute-start | bytes 614408 | tf_op jit(solution)/shard_map/while/body/eval_jaxpr/ppermute | solution.py:25
  164.8 9.6 %collective-permute-start.2 = (f32[2,200,128]{2,1,0:T(8,128)S(1)}, f32[2,200,128]{2,1,0:T(8,128)S(1)}, u32[]{:S(2)}, u32[]{:S(2)}) collective-permute-start(f32[2,200,128]{2,1,0:T(8,128)S(1)} %convolution_add_fusion.10), channel_id=1, source_target_pairs={{0,1},{1,2},{2,3},{3,4},{4,5},{5,6},{6,7},{8,9},{9,10},{10,11},{11... | collective-permute-start | bytes 614408 | tf_op jit(solution)/shard_map/while/body/eval_jaxpr/ppermute | solution.py:25
  174.9 8.7 %collective-permute-start.2 = (f32[2,200,128]{2,1,0:T(8,128)S(1)}, f32[2,200,128]{2,1,0:T(8,128)S(1)}, u32[]{:S(2)}, u32[]{:S(2)}) collective-permute-start(f32[2,200,128]{2,1,0:T(8,128)S(1)} %convolution_add_fusion.10), channel_id=1, source_target_pairs={{0,1},{1,2},{2,3},{3,4},{4,5},{5,6},{6,7},{8,9},{9,10},{10,11},{11... | collective-permute-start | bytes 614408 | tf_op jit(solution)/shard_map/while/body/eval_jaxpr/ppermute | solution.py:25
  184.1 8.4 %collective-permute-start.2 = (f32[2,200,128]{2,1,0:T(8,128)S(1)}, f32[2,200,128]{2,1,0:T(8,128)S(1)}, u32[]{:S(2)}, u32[]{:S(2)}) collective-permute-start(f32[2,200,128]{2,1,0:T(8,128)S(1)} %convolution_add_fusion.10), channel_id=1, source_target_pairs={{0,1},{1,2},{2,3},{3,4},{4,5},{5,6},{6,7},{8,9},{9,10},{10,11},{11... | collective-permute-start | bytes 614408 | tf_op jit(solution)/shard_map/while/body/eval_jaxpr/ppermute | solution.py:25
  193.0 8.6 %collective-permute-start.2 = (f32[2,200,128]{2,1,0:T(8,128)S(1)}, f32[2,200,128]{2,1,0:T(8,128)S(1)}, u32[]{:S(2)}, u32[]{:S(2)}) collective-permute-start(f32[2,200,128]{2,1,0:T(8,128)S(1)} %convolution_add_fusion.10), channel_id=1, source_target_pairs={{0,1},{1,2},{2,3},{3,4},{4,5},{5,6},{6,7},{8,9},{9,10},{10,11},{11... | collective-permute-start | bytes 614408 | tf_op jit(solution)/shard_map/while/body/eval_jaxpr/ppermute | solution.py:25
  202.1 8.6 %collective-permute-start.2 = (f32[2,200,128]{2,1,0:T(8,128)S(1)}, f32[2,200,128]{2,1,0:T(8,128)S(1)}, u32[]{:S(2)}, u32[]{:S(2)}) collective-permute-start(f32[2,200,128]{2,1,0:T(8,128)S(1)} %convolution_add_fusion.10), channel_id=1, source_target_pairs={{0,1},{1,2},{2,3},{3,4},{4,5},{5,6},{6,7},{8,9},{9,10},{10,11},{11... | collective-permute-start | bytes 614408 | tf_op jit(solution)/shard_map/while/body/eval_jaxpr/ppermute | solution.py:25
  211.1 8.6 %collective-permute-start.2 = (f32[2,200,128]{2,1,0:T(8,128)S(1)}, f32[2,200,128]{2,1,0:T(8,128)S(1)}, u32[]{:S(2)}, u32[]{:S(2)}) collective-permute-start(f32[2,200,128]{2,1,0:T(8,128)S(1)} %convolution_add_fusion.10), channel_id=1, source_target_pairs={{0,1},{1,2},{2,3},{3,4},{4,5},{5,6},{6,7},{8,9},{9,10},{10,11},{11... | collective-permute-start | bytes 614408 | tf_op jit(solution)/shard_map/while/body/eval_jaxpr/ppermute | solution.py:25
  222.0 9.0 %collective-permute-start.3 = (f32[2,200,128]{2,1,0:T(8,128)S(1)}, f32[2,200,128]{2,1,0:T(8,128)S(1)}, u32[]{:S(2)}, u32[]{:S(2)}) collective-permute-start(f32[2,200,128]{2,1,0:T(8,128)S(1)} %convolution_add_fusion.11), channel_id=1, source_target_pairs={{1,0},{2,1},{3,2},{4,3},{5,4},{6,5},{7,6},{9,8},{10,9},{11,10},{12... | collective-permute-start | bytes 614408 | tf_op jit(solution)/shard_map/while/body/eval_jaxpr/ppermute | solution.py:25
  231.6 11.0 %collective-permute-start.3 = (f32[2,200,128]{2,1,0:T(8,128)S(1)}, f32[2,200,128]{2,1,0:T(8,128)S(1)}, u32[]{:S(2)}, u32[]{:S(2)}) collective-permute-start(f32[2,200,128]{2,1,0:T(8,128)S(1)} %convolution_add_fusion.11), channel_id=1, source_target_pairs={{1,0},{2,1},{3,2},{4,3},{5,4},{6,5},{7,6},{9,8},{10,9},{11,10},{12... | collective-permute-start | bytes 614408 | tf_op jit(solution)/shard_map/while/body/eval_jaxpr/ppermute | solution.py:25
  243.1 10.0 %collective-permute-start.3 = (f32[2,200,128]{2,1,0:T(8,128)S(1)}, f32[2,200,128]{2,1,0:T(8,128)S(1)}, u32[]{:S(2)}, u32[]{:S(2)}) collective-permute-start(f32[2,200,128]{2,1,0:T(8,128)S(1)} %convolution_add_fusion.11), channel_id=1, source_target_pairs={{1,0},{2,1},{3,2},{4,3},{5,4},{6,5},{7,6},{9,8},{10,9},{11,10},{12... | collective-permute-start | bytes 614408 | tf_op jit(solution)/shard_map/while/body/eval_jaxpr/ppermute | solution.py:25
  253.6 9.2 %collective-permute-start.3 = (f32[2,200,128]{2,1,0:T(8,128)S(1)}, f32[2,200,128]{2,1,0:T(8,128)S(1)}, u32[]{:S(2)}, u32[]{:S(2)}) collective-permute-start(f32[2,200,128]{2,1,0:T(8,128)S(1)} %convolution_add_fusion.11), channel_id=1, source_target_pairs={{1,0},{2,1},{3,2},{4,3},{5,4},{6,5},{7,6},{9,8},{10,9},{11,10},{12... | collective-permute-start | bytes 614408 | tf_op jit(solution)/shard_map/while/body/eval_jaxpr/ppermute | solution.py:25
  263.3 8.6 %collective-permute-start.3 = (f32[2,200,128]{2,1,0:T(8,128)S(1)}, f32[2,200,128]{2,1,0:T(8,128)S(1)}, u32[]{:S(2)}, u32[]{:S(2)}) collective-permute-start(f32[2,200,128]{2,1,0:T(8,128)S(1)} %convolution_add_fusion.11), channel_id=1, source_target_pairs={{1,0},{2,1},{3,2},{4,3},{5,4},{6,5},{7,6},{9,8},{10,9},{11,10},{12... | collective-permute-start | bytes 614408 | tf_op jit(solution)/shard_map/while/body/eval_jaxpr/ppermute | solution.py:25
  272.3 8.6 %collective-permute-start.3 = (f32[2,200,128]{2,1,0:T(8,128)S(1)}, f32[2,200,128]{2,1,0:T(8,128)S(1)}, u32[]{:S(2)}, u32[]{:S(2)}) collective-permute-start(f32[2,200,128]{2,1,0:T(8,128)S(1)} %convolution_add_fusion.11), channel_id=1, source_target_pairs={{1,0},{2,1},{3,2},{4,3},{5,4},{6,5},{7,6},{9,8},{10,9},{11,10},{12... | collective-permute-start | bytes 614408 | tf_op jit(solution)/shard_map/while/body/eval_jaxpr/ppermute | solution.py:25
  281.4 8.6 %collective-permute-start.3 = (f32[2,200,128]{2,1,0:T(8,128)S(1)}, f32[2,200,128]{2,1,0:T(8,128)S(1)}, u32[]{:S(2)}, u32[]{:S(2)}) collective-permute-start(f32[2,200,128]{2,1,0:T(8,128)S(1)} %convolution_add_fusion.11), channel_id=1, source_target_pairs={{1,0},{2,1},{3,2},{4,3},{5,4},{6,5},{7,6},{9,8},{10,9},{11,10},{12... | collective-permute-start | bytes 614408 | tf_op jit(solution)/shard_map/while/body/eval_jaxpr/ppermute | solution.py:25
where the time goes:
time: 293 us; the launch traced here: 292 us
  waiting for transfers between devices  165 us (56%)
  starting transfers between devices  95.2 us (32%)
  matrix products  26.9 us (9%)
    ppermute x28, waiting for transfers between devices, from_behind(): lax.ppermute(value, axis, [(source, source + steps) for source in range(f...  159 us
    ppermute x28, starting transfers between devices, from_behind(): lax.ppermute(value, axis, [(source, source + steps) for source in range(f...  89.5 us
    dot_general x47, matrix products, apply_block(): jnp.einsum('aij,ajk->aik', inverse_row, operand, precision=lax.Precision....  26.9 us
  transfers between devices with their start and end apart: 30, of which 30 were waited for; matrix products, arithmetic and copies ran while one was open for 0% of the time, Pallas kernels for 0%

commit v1 on v0

v1 whole, which is shorter than its diff:
```python
import functools
import jax
import jax.numpy as jnp
from jax import lax
from jax.experimental import pallas as pl
from jax.experimental.pallas import tpu as pltpu
from jax.sharding import PartitionSpec as P

SWEEPS = 2
WIDTH = 2
MESH = pl.DeviceIdType.MESH


def split(value):
    high = value.astype(jnp.bfloat16)
    low = (value - high.astype(jnp.float32)).astype(jnp.bfloat16)
    return high, low


def keep(ref, index, value):
    high, low = split(value)
    ref[index + (0,)] = high
    ref[index + (1,)] = low


def apply(ref, index, operand):
    high, low = split(operand)
    left_high = ref[index + (0,)]
    left_low = ref[index + (1,)]
    dot = functools.partial(jnp.dot, preferred_element_type=jnp.float32)
    return dot(left_high, high) + (dot(left_high, low) + dot(left_low, high))


def kernel(
    segments,
    blocks,
    sources,
    inverse,
    radial,
    axial,
    out,
    plain,
    inner,
    outer,
    chain,
    line,
    value,
    field,
    low,
    high,
    arriving,
    leaving,
    send_sem,
    recv_sem,
    side_send,
    side_recv,
):
    stations, cells = sources.shape[:2]
    rad = lax.axis_index("rad")
    ax = lax.axis_index("ax")
    rad_up, rad_down = rad < segments - 1, rad > 0
    ax_up, ax_down = ax < blocks - 1, ax > 0

    barrier = pltpu.get_barrier_semaphore()
    neighbours = (
        (rad_up, {"rad": rad + 1}),
        (rad_down, {"rad": rad - 1}),
        (ax_up, {"ax": ax + 1}),
        (ax_down, {"ax": ax - 1}),
    )
    for exists, device in neighbours:

        @pl.when(exists)
        def _():
            pl.semaphore_signal(barrier, inc=1, device_id=device, device_id_type=MESH)

    peers = sum(jnp.where(exists, 1, 0) for exists, device in neighbours)
    pl.semaphore_wait(barrier, peers)

    def hop(number, station, step):
        return pltpu.make_async_remote_copy(
            src_ref=leaving.at[number, station],
            dst_ref=arriving.at[number, station],
            send_sem=send_sem.at[number, station],
            recv_sem=recv_sem.at[number, station],
            device_id={"rad": rad + step},
            device_id_type=MESH,
        )

    def side(direction):
        block = field.at[pl.ds(stations - WIDTH, WIDTH)] if direction == 0 else field.at[pl.ds(0, WIDTH)]
        return pltpu.make_async_remote_copy(
            src_ref=block,
            dst_ref=low if direction == 0 else high,
            send_sem=side_send.at[direction],
            recv_sem=side_recv.at[direction],
            device_id={"ax": ax + 1 if direction == 0 else ax - 1},
            device_id_type=MESH,
        )

    @pl.when(jnp.logical_not(rad_down))
    def _():
        for number in range(0, 2 * SWEEPS, 2):
            arriving[number] = jnp.zeros(arriving.shape[1:], jnp.float32)

    @pl.when(jnp.logical_not(rad_up))
    def _():
        for number in range(1, 2 * SWEEPS, 2):
            arriving[number] = jnp.zeros(arriving.shape[1:], jnp.float32)

    @pl.when(jnp.logical_not(ax_down))
    def _():
        low[...] = jnp.zeros(low.shape, jnp.float32)

    @pl.when(jnp.logical_not(ax_up))
    def _():
        high[...] = jnp.zeros(high.shape, jnp.float32)

    for a in range(stations):
        for c in range(cells):
            block = inverse[a, c]
            keep(plain, (a, c), block)
            keep(inner, (a, c), block * radial[a, c, 0:1, :])
            keep(outer, (a, c), block * radial[a, c, 1:2, :])
        product = -(inverse[a, 0] * radial[a, 0, 0:1, :])
        for c in range(1, cells):
            product = -apply(inner, (a, c), product)
        keep(chain, (0, a), product)
        product = -(inverse[a, cells - 1] * radial[a, cells - 1, 1:2, :])
        for c in reversed(range(cells - 1)):
            product = -apply(outer, (a, c), product)
        keep(chain, (1, a), product)

    for sweep in range(SWEEPS):
        if sweep == 0:
            source = sources
        else:

            @pl.when(ax_down)
            def _():
                side(0).wait_recv()

            @pl.when(ax_up)
            def _():
                side(1).wait_recv()

            for a in range(stations):
                for c in range(cells):
                    total = sources[a, c]
                    for j, place in enumerate((0, 1, 3, 4)):
                        at = a + place
                        if at < WIDTH:
                            other = low[at, c]
                        elif at < WIDTH + stations:
                            other = field[at - WIDTH, c]
                        else:
                            other = high[at - WIDTH - stations, c]
                        k = (a * cells + c) * 4 + j
                        total = total - axial[:, k : k + 1] * other
                    line[a, c] = total
            source = line
        number = 2 * sweep
        for a in range(stations):
            previous = apply(plain, (a, 0), source[a, 0])
            value[a, 0] = previous
            for c in range(1, cells):
                previous = apply(plain, (a, c), source[a, c]) - apply(inner, (a, c), previous)
                value[a, c] = previous
        for a in range(stations):

            @pl.when(rad_down)
            def _():
                hop(number, a, 1).wait_recv()

            @pl.when(rad_up)
            def _():
                leaving[number, a] = value[a, cells - 1] + apply(chain, (0, a), arriving[number, a])
                hop(number, a, 1).start()

        for a in range(stations):
            change = -apply(inner, (a, 0), arriving[number, a])
            value[a, 0] += change
            for c in range(1, cells):
                change = -apply(inner, (a, c), change)
                value[a, c] += change
        number = 2 * sweep + 1
        firsts = []
        for a in range(stations):
            following = value[a, cells - 1]
            for c in reversed(range(cells - 1)):
                following = value[a, c] - apply(outer, (a, c), following)
            firsts.append(following)
        for a in range(stations):

            @pl.when(rad_up)
            def _():
                hop(number, a, -1).wait_recv()

            @pl.when(rad_down)
            def _():
                leaving[number, a] = firsts[a] + apply(chain, (1, a), arriving[number, a])
                hop(number, a, -1).start()

        target = field if sweep < SWEEPS - 1 else out
        for a in range(stations):
            following = arriving[number, a]
            for c in reversed(range(cells)):
                following = value[a, c] - apply(outer, (a, c), following)
                target[a, c] = following
        if sweep < SWEEPS - 1:

            @pl.when(ax_up)
            def _():
                side(0).start()

            @pl.when(ax_down)
            def _():
                side(1).start()

    for number in range(2 * SWEEPS):
        for a in range(stations):

            @pl.when(rad_up if number % 2 == 0 else rad_down)
            def _():
                hop(number, a, 1 if number % 2 == 0 else -1).wait_send()

    @pl.when(ax_up)
    def _():
        side(0).wait_send()

    @pl.when(ax_down)
    def _():
        side(1).wait_send()


def on_device(segments, blocks, sources, block_inverse, radial_coupling, axial_coupling):
    stations, cells, species, columns = sources.shape
    axial = axial_coupling.reshape(-1, species).T
    matrix = pltpu.VMEM((stations, cells, 2, species, species), jnp.bfloat16)
    grid = pltpu.VMEM((stations, cells, species, columns), jnp.float32)
    edge = pltpu.VMEM((WIDTH, cells, species, columns), jnp.float32)
    slots = pltpu.VMEM((2 * SWEEPS, stations, species, columns), jnp.float32)
    spec = pl.BlockSpec(memory_space=pltpu.VMEM)
    return pl.pallas_call(
        functools.partial(kernel, segments, blocks),
        out_shape=jax.ShapeDtypeStruct(sources.shape, jnp.float32),
        in_specs=[spec] * 4,
        out_specs=spec,
        scratch_shapes=[
            matrix,
            matrix,
            matrix,
            pltpu.VMEM((2, stations, 2, species, species), jnp.bfloat16),
            grid,
            grid,
            grid,
            edge,
            edge,
            slots,
            slots,
            pltpu.SemaphoreType.DMA((2 * SWEEPS, stations)),
            pltpu.SemaphoreType.DMA((2 * SWEEPS, stations)),
            pltpu.SemaphoreType.DMA((2,)),
            pltpu.SemaphoreType.DMA((2,)),
        ],
        compiler_params=pltpu.CompilerParams(
            collective_id=0, has_side_effects=True, vmem_limit_bytes=40 << 20
        ),
    )(sources, block_inverse, radial_coupling, axial)


def solution(mesh):
    placed = P("ax", "rad", None, None)
    return jax.shard_map(
        functools.partial(on_device, mesh.shape["rad"], mesh.shape["ax"]),
        mesh=mesh,
        in_specs=(placed,) * 4,
        out_specs=placed,
        check_vma=False,
    )
```

time: 293 us -> 141 us (0.48)
  the two profiles are of different devices: /device:TPU:6 before, /device:TPU:0 now
where the time goes in v1:
time: 141 us
  Pallas kernels  136 us (96%)
  local copies, waits for them, and re-layouts  4.32 us (3%)
    pallas_call x1, Pallas kernels, on_device(): pl.pallas_call(functools.partial(kernel, segments, blocks), out_shape=jax...  136 us
    unnamed x7, local copies, waits for them, and re-layouts  3.5 us

profile of v1, /device:TPU:0, one launch (start us, length us, event | category | flops | bytes accessed | tf_op | source)
XLA Modules:
  0.0 140.6 jit_solution(15348807654476648392)
XLA Ops:
  0.0 0.7 reshape.3
  0.7 0.0 copy-start.2
  0.7 0.1 copy.6
  0.8 0.6 copy-done.2
  1.4 0.0 copy-start
  1.4 1.1 copy-done
  2.6 0.0 copy-start.1
  2.6 1.0 copy-done.1
  3.6 136.2 %shard_map.46 = f32[2,2,200,128]{3,2,1,0:T(8,128)S(1)} custom-call(f32[2,2,200,128]{3,2,1,0:T(8,128)S(1)} %copy-done.1, f32[2,2,200,200]{3,2,1,0:T(8,128)S(1)} %copy-done, f32[2,2,2,200]{3,2,1,0:T(2,128)S(1)} %copy-done.2, f32[200,16]{1,0:T(8,128)S(1)} %bitcast.1), custom_call_target="tpu_custom_call" | custom-call | tf_op jit(solution)/shard_map/pallas_call | solution.py:244
  139.8 0.8 copy.8
Async XLA Ops:
  0.7 0.7 copy-start.2
  1.4 1.1 copy-start
  2.6 1.0 copy-start.1

commit v2 on v1

v2 whole, which is shorter than its diff:
```python
import functools
import jax
import jax.numpy as jnp
from jax import lax
from jax.experimental import pallas as pl
from jax.experimental.pallas import tpu as pltpu
from jax.sharding import PartitionSpec as P

SWEEPS = 2
WIDTH = 2
MESH = pl.DeviceIdType.MESH


def split(value):
    high = value.astype(jnp.bfloat16)
    low = (value - high.astype(jnp.float32)).astype(jnp.bfloat16)
    return high, low


def keep(ref, index, value):
    high, low = split(value)
    ref[index + (0,)] = high
    ref[index + (1,)] = low


def apply(ref, index, operand):
    high, low = split(operand)
    left_high = ref[index + (0,)]
    left_low = ref[index + (1,)]
    dot = functools.partial(jnp.dot, preferred_element_type=jnp.float32)
    return dot(left_high, high) + (dot(left_high, low) + dot(left_low, high))


def kernel(
    segments,
    blocks,
    sources,
    inverse,
    radial,
    axial,
    out,
    plain,
    inner,
    outer,
    pair,
    sent_matrix,
    got_matrix,
    own_matrix,
    line,
    value,
    field,
    low,
    high,
    sent,
    got,
    local,
    arriving,
    leaving,
    matrix_send,
    matrix_recv,
    pair_send,
    pair_recv,
    hop_send,
    hop_recv,
    side_send,
    side_recv,
):
    stations, cells = sources.shape[:2]
    half = stations // 2
    rad = lax.axis_index("rad")
    ax = lax.axis_index("ax")
    parity = lax.rem(rad, 2)
    is_first = parity == 0
    top, bottom = rad >= segments - 2, rad < 2
    has_up, has_down = jnp.logical_not(top), jnp.logical_not(bottom)
    ax_up, ax_down = ax < blocks - 1, ax > 0
    partner = {"rad": rad + 1 - 2 * parity}
    mine = [parity * half + i for i in range(half)]
    other = [(1 - parity) * half + i for i in range(half)]

    barrier = pltpu.get_barrier_semaphore()
    neighbours = (
        (has_up, {"rad": rad + 2}),
        (has_down, {"rad": rad - 2}),
        (ax_up, {"ax": ax + 1}),
        (ax_down, {"ax": ax - 1}),
    )
    pl.semaphore_signal(barrier, inc=1, device_id=partner, device_id_type=MESH)
    for exists, device in neighbours:

        @pl.when(exists)
        def _():
            pl.semaphore_signal(barrier, inc=1, device_id=device, device_id_type=MESH)

    def remote(source, target, send_sem, recv_sem, device):
        return pltpu.make_async_remote_copy(
            src_ref=source,
            dst_ref=target,
            send_sem=send_sem,
            recv_sem=recv_sem,
            device_id=device,
            device_id_type=MESH,
        )

    def swap_matrix(kind, i):
        at = (kind, i)
        return remote(
            sent_matrix.at[at], got_matrix.at[at], matrix_send.at[at], matrix_recv.at[at], partner
        )

    def swap(sweep, kind, i):
        at = (sweep, kind, i)
        return remote(sent.at[at], got.at[at], pair_send.at[at], pair_recv.at[at], partner)

    def hop(number, i):
        at = (number, i)
        device = {"rad": rad + 2 if number % 2 == 0 else rad - 2}
        return remote(leaving.at[at], arriving.at[at], hop_send.at[at], hop_recv.at[at], device)

    def side(direction, station):
        at = (direction, station)
        device = {"ax": ax + 1 if direction == 0 else ax - 1}
        target = low if direction == 0 else high
        return remote(
            field.at[station], target.at[station], side_send.at[at], side_recv.at[at], device
        )

    @pl.when(bottom)
    def _():
        for number in range(0, 2 * SWEEPS, 2):
            arriving[number] = jnp.zeros(arriving.shape[1:], jnp.float32)

    @pl.when(top)
    def _():
        for number in range(1, 2 * SWEEPS, 2):
            arriving[number] = jnp.zeros(arriving.shape[1:], jnp.float32)

    @pl.when(jnp.logical_not(ax_down))
    def _():
        low[...] = jnp.zeros(low.shape, jnp.float32)

    @pl.when(jnp.logical_not(ax_up))
    def _():
        high[...] = jnp.zeros(high.shape, jnp.float32)

    def forms(a):
        for c in range(cells):
            block = inverse[a, c]
            keep(plain, (a, c), block)
            keep(inner, (a, c), block * radial[a, c, 0:1, :])
            keep(outer, (a, c), block * radial[a, c, 1:2, :])

    def inner_responses(a):
        answers = [-(inverse[a, 0] * radial[a, 0, 0:1, :])]
        for c in range(1, cells):
            answers.append(-apply(inner, (a, c), answers[-1]))
        return answers

    def other_responses(a, answers):
        turned = answers[-1]
        product = -(inverse[a, cells - 1] * radial[a, cells - 1, 1:2, :])
        for c in reversed(range(cells - 1)):
            turned = answers[c] - apply(outer, (a, c), turned)
            product = -apply(outer, (a, c), product)
        return turned, product

    def first_guess(source, a):
        previous = apply(plain, (a, 0), source[a, 0])
        value[a, 0] = previous
        for c in range(1, cells):
            previous = apply(plain, (a, c), source[a, c]) - apply(inner, (a, c), previous)
            value[a, c] = previous
        return previous

    def first_turn(a):
        following = value[a, cells - 1]
        for c in reversed(range(cells - 1)):
            following = value[a, c] - apply(outer, (a, c), following)
        return following

    def inner_update(a, incoming):
        change = -apply(inner, (a, 0), incoming)
        value[a, 0] += change
        for c in range(1, cells):
            change = -apply(inner, (a, c), change)
            value[a, c] += change

    def outer_finish(target, a, incoming):
        following = incoming
        for c in reversed(range(cells)):
            following = value[a, c] - apply(outer, (a, c), following)
            target[a, c] = following

    def ordered(own, foreign):
        return jnp.where(is_first, own, foreign), jnp.where(is_first, foreign, own)

    for i in range(half):
        forms(other[i])
    kept = [inner_responses(other[i]) for i in range(half)]
    for i in range(half):
        sent_matrix[0, i] = kept[i][-1]
    peers = 1 + sum(jnp.where(exists, 1, 0) for exists, device in neighbours)
    pl.semaphore_wait(barrier, peers)
    for i in range(half):
        swap_matrix(0, i).start()

    for sweep in range(SWEEPS):
        if sweep == 0:
            source = sources
        else:
            for direction, exists in ((0, ax_down), (1, ax_up)):

                @pl.when(exists)
                def _():
                    for a in mine + other:
                        side(direction, a).wait_recv()

            for a in range(stations):
                for c in range(cells):
                    total = sources[a, c]
                    for j, place in enumerate((0, 1, 3, 4)):
                        at = a + place
                        if at < WIDTH:
                            near = low[at, c]
                        elif at < WIDTH + stations:
                            near = field[at - WIDTH, c]
                        else:
                            near = high[at - WIDTH - stations, c]
                        k = (a * cells + c) * 4 + j
                        total = total - axial[:, k : k + 1] * near
                    line[a, c] = total
            source = line

        for i in range(half):
            sent[sweep, 0, i] = first_guess(source, other[i])
            swap(sweep, 0, i).start()
        for i in range(half):
            sent[sweep, 1, i] = first_turn(other[i])
            swap(sweep, 1, i).start()
        if sweep == 0:
            for i in range(half):
                turned, product = other_responses(other[i], kept[i])
                sent_matrix[1, i] = turned
                swap_matrix(1, i).start()
                sent_matrix[2, i] = product
                swap_matrix(2, i).start()
            for i in range(half):
                a = mine[i]
                forms(a)
                answers = inner_responses(a)
                turned, product = other_responses(a, answers)
                own_matrix[0, i] = answers[-1]
                own_matrix[1, i] = turned
                own_matrix[2, i] = product
        for i in range(half):
            local[0, i] = first_guess(source, mine[i])
            local[1, i] = first_turn(mine[i])
        if sweep == 0:
            for i in range(half):
                swap_matrix(0, i).wait_recv()
                near, far = ordered(own_matrix[0, i], got_matrix[0, i])
                keep(pair, (0, i), near)
                keep(pair, (1, i), far)
                keep(pair, (2, i), apply(pair, (1, i), near))

        up, down = 2 * sweep, 2 * sweep + 1
        for i in range(half):
            swap(sweep, 0, i).wait_recv()
            near, far = ordered(local[0, i], got[sweep, 0, i])
            whole = far + apply(pair, (1, i), near)

            @pl.when(has_down)
            def _():
                hop(up, i).wait_recv()

            incoming = arriving[up, i]

            @pl.when(has_up)
            def _():
                leaving[up, i] = whole + apply(pair, (2, i), incoming)
                hop(up, i).start()

            middle = near + apply(pair, (0, i), incoming)
            own_in, foreign_in = ordered(incoming, middle)
            local[2, i] = own_in
            sent[sweep, 2, i] = foreign_in
            swap(sweep, 2, i).start()
            if sweep == 0:
                swap_matrix(1, i).wait_recv()
                swap_matrix(2, i).wait_recv()
                near, far = ordered(own_matrix[1, i], got_matrix[1, i])
                keep(pair, (3, i), near)
                keep(pair, (4, i), far)
                near, far = ordered(own_matrix[2, i], got_matrix[2, i])
                keep(pair, (5, i), near)
                keep(pair, (6, i), far)
                keep(pair, (7, i), apply(pair, (5, i), far))
            swap(sweep, 1, i).wait_recv()
            near, far = ordered(local[1, i], got[sweep, 1, i])
            far = far + apply(pair, (4, i), middle)
            whole = near + apply(pair, (3, i), incoming) + apply(pair, (5, i), far)
            local[3, i] = far
            local[4, i] = whole

            @pl.when(top)
            def _():
                leaving[down, i] = whole
                hop(down, i).start()

        for i in range(half):
            inner_update(mine[i], local[2, i])
        for i in range(half):
            swap(sweep, 2, i).wait_recv()
            inner_update(other[i], got[sweep, 2, i])
        for i in range(half):

            @pl.when(has_up)
            def _():
                hop(down, i).wait_recv()

            incoming = arriving[down, i]

            @pl.when(jnp.logical_and(has_up, has_down))
            def _():
                leaving[down, i] = local[4, i] + apply(pair, (7, i), incoming)
                hop(down, i).start()

            middle = local[3, i] + apply(pair, (6, i), incoming)
            foreign_in, own_in = ordered(incoming, middle)
            sent[sweep, 3, i] = foreign_in
            swap(sweep, 3, i).start()
            local[2, i] = own_in

        target = field if sweep < SWEEPS - 1 else out

        def share(a):
            for direction, exists in ((0, ax_up), (1, ax_down)):

                @pl.when(exists)
                def _():
                    side(direction, a).start()

        for i in range(half):
            outer_finish(target, mine[i], local[2, i])
            if sweep < SWEEPS - 1:
                share(mine[i])
        for i in range(half):
            swap(sweep, 3, i).wait_recv()
            outer_finish(target, other[i], got[sweep, 3, i])
            if sweep < SWEEPS - 1:
                share(other[i])

    for i in range(half):
        for kind in range(3):
            swap_matrix(kind, i).wait_send()
        for sweep in range(SWEEPS):
            for kind in range(4):
                swap(sweep, kind, i).wait_send()

            @pl.when(has_up)
            def _():
                hop(2 * sweep, i).wait_send()

            @pl.when(has_down)
            def _():
                hop(2 * sweep + 1, i).wait_send()

    for direction, exists in ((0, ax_up), (1, ax_down)):

        @pl.when(exists)
        def _():
            for a in mine + other:
                side(direction, a).wait_send()


def on_device(segments, blocks, sources, block_inverse, radial_coupling, axial_coupling):
    stations, cells, species, columns = sources.shape
    half = stations // 2
    assert segments % 2 == 0 and segments >= 4 and stations == WIDTH
    axial = axial_coupling.reshape(-1, species).T
    matrix = pltpu.VMEM((stations, cells, 2, species, species), jnp.bfloat16)
    square = pltpu.VMEM((3, half, species, species), jnp.float32)
    grid = pltpu.VMEM((stations, cells, species, columns), jnp.float32)
    swaps = pltpu.VMEM((SWEEPS, 4, half, species, columns), jnp.float32)
    slots = pltpu.VMEM((2 * SWEEPS, half, species, columns), jnp.float32)
    sems = [
        pltpu.SemaphoreType.DMA(shape)
        for shape in ((3, half), (SWEEPS, 4, half), (2 * SWEEPS, half), (2, stations))
        for side in range(2)
    ]
    spec = pl.BlockSpec(memory_space=pltpu.VMEM)
    return pl.pallas_call(
        functools.partial(kernel, segments, blocks),
        out_shape=jax.ShapeDtypeStruct(sources.shape, jnp.float32),
        in_specs=[spec] * 4,
        out_specs=spec,
        scratch_shapes=[
            matrix,
            matrix,
            matrix,
            pltpu.VMEM((8, half, 2, species, species), jnp.bfloat16),
            square,
            square,
            square,
            grid,
            grid,
            grid,
            grid,
            grid,
            swaps,
            swaps,
            pltpu.VMEM((5, half, species, columns), jnp.float32),
            slots,
            slots,
            *sems,
        ],
        compiler_params=pltpu.CompilerParams(
            collective_id=0, has_side_effects=True, vmem_limit_bytes=48 << 20
        ),
    )(sources, block_inverse, radial_coupling, axial)


def solution(mesh):
    placed = P("ax", "rad", None, None)
    return jax.shard_map(
        functools.partial(on_device, mesh.shape["rad"], mesh.shape["ax"]),
        mesh=mesh,
        in_specs=(placed,) * 4,
        out_specs=placed,
        check_vma=False,
    )
```

time: 141 us -> 80.8 us (0.57)
  Pallas kernels: 136 us -> 76.2 us
    pallas_call x1, Pallas kernels: 136 us -> 76.2 us  [on_device(): pl.pallas_call(functools.partial(kernel, segments, blocks), out_shape=jax...]
where the time goes in v2:
time: 80.8 us; the launch traced here: 80.5 us
  Pallas kernels  76.2 us (94%)
  local copies, waits for them, and re-layouts  4.32 us (5%)
    pallas_call x1, Pallas kernels, on_device(): pl.pallas_call(functools.partial(kernel, segments, blocks), out_shape=jax...  76.2 us
    unnamed x7, local copies, waits for them, and re-layouts  3.5 us

profile of v2, /device:TPU:0, one launch (start us, length us, event | category | flops | bytes accessed | tf_op | source)
XLA Modules:
  0.0 80.5 jit_solution(15125557734499300011)
XLA Ops:
  0.0 0.7 reshape.3
  0.7 0.0 copy-start.2
  0.7 0.1 copy.6
  0.8 0.6 copy-done.2
  1.4 0.0 copy-start
  1.4 1.1 %copy-done = f32[2,2,200,200]{3,2,1,0:T(8,128)S(1)} copy-done((f32[2,2,200,200]{3,2,1,0:T(8,128)S(1)}, f32[2,2,200,200]{3,2,1,0:T(8,128)}, u32[]{:S(2)}) %copy-start) | copy-done | bytes 640024
  2.6 0.0 copy-start.1
  2.6 1.0 %copy-done.1 = f32[2,2,200,128]{3,2,1,0:T(8,128)S(1)} copy-done((f32[2,2,200,128]{3,2,1,0:T(8,128)S(1)}, f32[2,2,200,128]{3,2,1,0:T(8,128)}, u32[]{:S(2)}) %copy-start.1) | copy-done | bytes 409624
  3.6 76.2 %shard_map.46 = f32[2,2,200,128]{3,2,1,0:T(8,128)S(1)} custom-call(f32[2,2,200,128]{3,2,1,0:T(8,128)S(1)} %copy-done.1, f32[2,2,200,200]{3,2,1,0:T(8,128)S(1)} %copy-done, f32[2,2,2,200]{3,2,1,0:T(2,128)S(1)} %copy-done.2, f32[200,16]{1,0:T(8,128)S(1)} %bitcast.1), custom_call_target="tpu_custom_call" | custom-call | tf_op jit(solution)/shard_map/pallas_call | solution.py:392
  79.7 0.8 copy.8
Async XLA Ops:
  0.7 0.7 copy-start.2
  1.4 1.1 %copy-start = (f32[2,2,200,200]{3,2,1,0:T(8,128)S(1)}, f32[2,2,200,200]{3,2,1,0:T(8,128)}, u32[]{:S(2)}) copy-start(f32[2,2,200,200]{3,2,1,0:T(8,128)} %inverse.1) | copy-start | bytes 1920004
  2.6 1.0 %copy-start.1 = (f32[2,2,200,128]{3,2,1,0:T(8,128)S(1)}, f32[2,2,200,128]{3,2,1,0:T(8,128)}, u32[]{:S(2)}) copy-start(f32[2,2,200,128]{3,2,1,0:T(8,128)} %sources.1) | copy-start | bytes 1228804

commit v3 on v2

--- a/solution.py
+++ b/solution.py
@@ -46,6 +46,8 @@
     sent_matrix,
     got_matrix,
     own_matrix,
+    fold_out,
+    fold_in,
     line,
     value,
     field,
@@ -56,6 +58,8 @@
     local,
     arriving,
     leaving,
+    early_out,
+    early_in,
     matrix_send,
     matrix_recv,
     pair_send,
@@ -64,6 +68,10 @@
     hop_recv,
     side_send,
     side_recv,
+    early_send,
+    early_recv,
+    fold_send,
+    fold_recv,
 ):
     stations, cells = sources.shape[:2]
     half = stations // 2
@@ -72,6 +80,8 @@
     parity = lax.rem(rad, 2)
     is_first = parity == 0
     top, bottom = rad >= segments - 2, rad < 2
+    turn = jnp.logical_and(rad >= segments - 4, rad < segments - 2)
+    below = rad < segments - 4
     has_up, has_down = jnp.logical_not(top), jnp.logical_not(bottom)
     ax_up, ax_down = ax < blocks - 1, ax > 0
     partner = {"rad": rad + 1 - 2 * parity}
@@ -116,6 +126,16 @@
         at = (number, i)
         device = {"rad": rad + 2 if number % 2 == 0 else rad - 2}
         return remote(leaving.at[at], arriving.at[at], hop_send.at[at], hop_recv.at[at], device)
+
+    def early(sweep, i):
+        at = (sweep, i)
+        device = {"rad": jnp.where(top, rad - 2, rad + 2)}
+        return remote(early_out.at[at], early_in.at[at], early_send.at[at], early_recv.at[at], device)
+
+    def fold(i):
+        return remote(
+            fold_out.at[i], fold_in.at[i], fold_send.at[i], fold_recv.at[i], {"rad": rad - 2}
+        )
 
     def side(direction, station):
         at = (direction, station)
@@ -261,24 +281,102 @@
                 near, far = ordered(own_matrix[0, i], got_matrix[0, i])
                 keep(pair, (0, i), near)
                 keep(pair, (1, i), far)
-                keep(pair, (2, i), apply(pair, (1, i), near))
 
         up, down = 2 * sweep, 2 * sweep + 1
+
+        def late_forms(i):
+            swap_matrix(1, i).wait_recv()
+            swap_matrix(2, i).wait_recv()
+            near, far = ordered(own_matrix[1, i], got_matrix[1, i])
+            keep(pair, (3, i), near)
+            keep(pair, (4, i), far)
+            near, far = ordered(own_matrix[2, i], got_matrix[2, i])
+            keep(pair, (5, i), near)
+            keep(pair, (6, i), far)
+            keep(pair, (7, i), apply(pair, (5, i), far))
+
+        def whole_response(i):
+            first, _ = ordered(own_matrix[0, i], got_matrix[0, i])
+            turned, _ = ordered(own_matrix[1, i], got_matrix[1, i])
+            return turned + apply(pair, (5, i), apply(pair, (4, i), first))
+
         for i in range(half):
             swap(sweep, 0, i).wait_recv()
             near, far = ordered(local[0, i], got[sweep, 0, i])
             whole = far + apply(pair, (1, i), near)
 
+            @pl.when(turn)
+            def _():
+                early_out[sweep, i] = whole
+                early(sweep, i).start()
+
+            @pl.when(bottom)
+            def _():
+                leaving[up, i] = whole
+                hop(up, i).start()
+
+            if sweep == 0:
+                first, _ = ordered(own_matrix[0, i], got_matrix[0, i])
+                product = apply(pair, (1, i), first)
+                fold_out[i] = product
+                keep(pair, (2, i), product)
+
+                @pl.when(top)
+                def _():
+                    late_forms(i)
+                    response = whole_response(i)
+                    fold_out[i] = response
+                    fold(i).start()
+                    keep(pair, (8, i), response)
+
+                @pl.when(turn)
+                def _():
+                    late_forms(i)
+                    response = whole_response(i)
+                    fold(i).wait_recv()
+                    keep(pair, (9, i), fold_in[i])
+                    beyond = apply(pair, (9, i), fold_out[i])
+                    keep(pair, (8, i), beyond)
+                    keep(pair, (9, i), response + apply(pair, (7, i), beyond))
+
+            swap(sweep, 1, i).wait_recv()
+            near_turn, far_turn = ordered(local[1, i], got[sweep, 1, i])
+
+            def unfed():
+                return near_turn + apply(pair, (5, i), far_turn + apply(pair, (4, i), near))
+
+            @pl.when(top)
+            def _():
+                guess = unfed()
+                early(sweep, i).wait_recv()
+                early_out[sweep, i] = guess + apply(pair, (8, i), early_in[sweep, i])
+                early(sweep, i).start()
+
+            @pl.when(turn)
+            def _():
+                guess = unfed()
+                early(sweep, i).wait_recv()
+                local[4, i] = guess + apply(pair, (7, i), early_in[sweep, i])
+
             @pl.when(has_down)
             def _():
                 hop(up, i).wait_recv()
 
             incoming = arriving[up, i]
 
-            @pl.when(has_up)
+            @pl.when(turn)
+            def _():
+                leaving[down, i] = local[4, i] + apply(pair, (9, i), incoming)
+                hop(down, i).start()
+
+            @pl.when(jnp.logical_and(has_up, has_down))
             def _():
                 leaving[up, i] = whole + apply(pair, (2, i), incoming)
                 hop(up, i).start()
+
+            @pl.when(turn)
+            def _():
+                arriving[down, i] = early_in[sweep, i] + apply(pair, (8, i), incoming)
 
             middle = near + apply(pair, (0, i), incoming)
             own_in, foreign_in = ordered(incoming, middle)
@@ -286,26 +384,17 @@
             sent[sweep, 2, i] = foreign_in
             swap(sweep, 2, i).start()
             if sweep == 0:
-                swap_matrix(1, i).wait_recv()
-                swap_matrix(2, i).wait_recv()
-                near, far = ordered(own_matrix[1, i], got_matrix[1, i])
-                keep(pair, (3, i), near)
-                keep(pair, (4, i), far)
-                near, far = ordered(own_matrix[2, i], got_matrix[2, i])
-                keep(pair, (5, i), near)
-                keep(pair, (6, i), far)
-                keep(pair, (7, i), apply(pair, (5, i), far))
-            swap(sweep, 1, i).wait_recv()
-            near, far = ordered(local[1, i], got[sweep, 1, i])
-            far = far + apply(pair, (4, i), middle)
-            whole = near + apply(pair, (3, i), incoming) + apply(pair, (5, i), far)
+
+                @pl.when(below)
+                def _():
+                    late_forms(i)
+
+            far = far_turn + apply(pair, (4, i), middle)
             local[3, i] = far
-            local[4, i] = whole
-
-            @pl.when(top)
-            def _():
-                leaving[down, i] = whole
-                hop(down, i).start()
+
+            @pl.when(below)
+            def _():
+                local[4, i] = near_turn + apply(pair, (3, i), incoming) + apply(pair, (5, i), far)
 
         for i in range(half):
             inner_update(mine[i], local[2, i])
@@ -314,13 +403,13 @@
             inner_update(other[i], got[sweep, 2, i])
         for i in range(half):
 
-            @pl.when(has_up)
+            @pl.when(below)
             def _():
                 hop(down, i).wait_recv()
 
             incoming = arriving[down, i]
 
-            @pl.when(jnp.logical_and(has_up, has_down))
+            @pl.when(jnp.logical_and(below, has_down))
             def _():
                 leaving[down, i] = local[4, i] + apply(pair, (7, i), incoming)
                 hop(down, i).start()
@@ -361,9 +450,17 @@
             def _():
                 hop(2 * sweep, i).wait_send()
 
-            @pl.when(has_down)
+            @pl.when(jnp.logical_and(has_up, has_down))
             def _():
                 hop(2 * sweep + 1, i).wait_send()
+
+            @pl.when(jnp.logical_not(below))
+            def _():
+                early(sweep, i).wait_send()
+
+        @pl.when(top)
+        def _():
+            fold(i).wait_send()
 
     for direction, exists in ((0, ax_up), (1, ax_down)):
 
@@ -376,16 +473,18 @@
 def on_device(segments, blocks, sources, block_inverse, radial_coupling, axial_coupling):
     stations, cells, species, columns = sources.shape
     half = stations // 2
-    assert segments % 2 == 0 and segments >= 4 and stations == WIDTH
+    assert segments % 2 == 0 and segments >= 6 and stations == WIDTH
     axial = axial_coupling.reshape(-1, species).T
     matrix = pltpu.VMEM((stations, cells, 2, species, species), jnp.bfloat16)
     square = pltpu.VMEM((3, half, species, species), jnp.float32)
     grid = pltpu.VMEM((stations, cells, species, columns), jnp.float32)
     swaps = pltpu.VMEM((SWEEPS, 4, half, species, columns), jnp.float32)
     slots = pltpu.VMEM((2 * SWEEPS, half, species, columns), jnp.float32)
+    earlies = pltpu.VMEM((SWEEPS, half, species, columns), jnp.float32)
+    fold = pltpu.VMEM((half, species, species), jnp.float32)
     sems = [
         pltpu.SemaphoreType.DMA(shape)
-        for shape in ((3, half), (SWEEPS, 4, half), (2 * SWEEPS, half), (2, stations))
+        for shape in ((3, half), (SWEEPS, 4, half), (2 * SWEEPS, half), (2, stations), (SWEEPS, half), (half,))
         for side in range(2)
     ]
     spec = pl.BlockSpec(memory_space=pltpu.VMEM)
@@ -398,10 +497,12 @@
             matrix,
             matrix,
             matrix,
-            pltpu.VMEM((8, half, 2, species, species), jnp.bfloat16),
+            pltpu.VMEM((10, half, 2, species, species), jnp.bfloat16),
             square,
             square,
             square,
+            fold,
+            fold,
             grid,
             grid,
             grid,
@@ -412,6 +513,8 @@
             pltpu.VMEM((5, half, species, columns), jnp.float32),
             slots,
             slots,
+            earlies,
+            earlies,
             *sems,
         ],
         compiler_params=pltpu.CompilerParams(

time: 80.8 us -> 76.4 us (0.946)
  Pallas kernels: 76.2 us -> 71.4 us
    pallas_call x1, Pallas kernels: 76.2 us -> 71.4 us  [on_device(): pl.pallas_call(functools.partial(kernel, segments, blocks), out_shape=jax...]
where the time goes in v3:
time: 76.4 us; the launch traced here: 75.7 us
  Pallas kernels  71.4 us (93%)
  local copies, waits for them, and re-layouts  4.32 us (6%)
    pallas_call x1, Pallas kernels, on_device(): pl.pallas_call(functools.partial(kernel, segments, blocks), out_shape=jax...  71.4 us
    unnamed x7, local copies, waits for them, and re-layouts  3.5 us

profile of v3, /device:TPU:0, one launch (start us, length us, event | category | flops | bytes accessed | tf_op | source)
XLA Modules:
  0.0 75.7 jit_solution(6350396624203723323)
XLA Ops:
  0.0 0.7 reshape.3
  0.7 0.0 copy-start.2
  0.7 0.1 copy.6
  0.8 0.6 copy-done.2
  1.4 0.0 copy-start
  1.4 1.1 %copy-done = f32[2,2,200,200]{3,2,1,0:T(8,128)S(1)} copy-done((f32[2,2,200,200]{3,2,1,0:T(8,128)S(1)}, f32[2,2,200,200]{3,2,1,0:T(8,128)}, u32[]{:S(2)}) %copy-start) | copy-done | bytes 640024
  2.6 0.0 copy-start.1
  2.6 1.0 %copy-done.1 = f32[2,2,200,128]{3,2,1,0:T(8,128)S(1)} copy-done((f32[2,2,200,128]{3,2,1,0:T(8,128)S(1)}, f32[2,2,200,128]{3,2,1,0:T(8,128)}, u32[]{:S(2)}) %copy-start.1) | copy-done | bytes 409624
  3.6 71.4 %shard_map.46 = f32[2,2,200,128]{3,2,1,0:T(8,128)S(1)} custom-call(f32[2,2,200,128]{3,2,1,0:T(8,128)S(1)} %copy-done.1, f32[2,2,200,200]{3,2,1,0:T(8,128)S(1)} %copy-done, f32[2,2,2,200]{3,2,1,0:T(2,128)S(1)} %copy-done.2, f32[200,16]{1,0:T(8,128)S(1)} %bitcast.1), custom_call_target="tpu_custom_call" | custom-call | tf_op jit(solution)/shard_map/pallas_call | solution.py:491
  75.0 0.8 copy.8
Async XLA Ops:
  0.7 0.7 copy-start.2
  1.4 1.1 %copy-start = (f32[2,2,200,200]{3,2,1,0:T(8,128)S(1)}, f32[2,2,200,200]{3,2,1,0:T(8,128)}, u32[]{:S(2)}) copy-start(f32[2,2,200,200]{3,2,1,0:T(8,128)} %inverse.1) | copy-start | bytes 1920004
  2.6 1.0 %copy-start.1 = (f32[2,2,200,128]{3,2,1,0:T(8,128)S(1)}, f32[2,2,200,128]{3,2,1,0:T(8,128)}, u32[]{:S(2)}) copy-start(f32[2,2,200,128]{3,2,1,0:T(8,128)} %sources.1) | copy-start | bytes 1228804

commit v4 on v3

--- a/solution.py
+++ b/solution.py
@@ -43,7 +43,10 @@
     inner,
     outer,
     pair,
-    sent_matrix,
+    far_inner,
+    far_outer,
+    got_block,
+    got_radial,
     got_matrix,
     own_matrix,
     fold_out,
@@ -112,11 +115,15 @@
             device_id_type=MESH,
         )
 
-    def swap_matrix(kind, i):
-        at = (kind, i)
-        return remote(
-            sent_matrix.at[at], got_matrix.at[at], matrix_send.at[at], matrix_recv.at[at], partner
-        )
+    def swap_block(i, c):
+        at = (c, i)
+        source = inverse.at[other[i], c]
+        return remote(source, got_block.at[i, c], matrix_send.at[at], matrix_recv.at[at], partner)
+
+    def swap_radial(i):
+        at = (cells, i)
+        source = radial.at[other[i]]
+        return remote(source, got_radial.at[i], matrix_send.at[at], matrix_recv.at[at], partner)
 
     def swap(sweep, kind, i):
         at = (sweep, kind, i)
@@ -170,19 +177,18 @@
             keep(inner, (a, c), block * radial[a, c, 0:1, :])
             keep(outer, (a, c), block * radial[a, c, 1:2, :])
 
-    def inner_responses(a):
-        answers = [-(inverse[a, 0] * radial[a, 0, 0:1, :])]
+    def responses(target, i, block, rates, inner, outer, a):
+        answers = [-(block[a, 0] * rates[a, 0, 0:1, :])]
         for c in range(1, cells):
             answers.append(-apply(inner, (a, c), answers[-1]))
-        return answers
-
-    def other_responses(a, answers):
         turned = answers[-1]
-        product = -(inverse[a, cells - 1] * radial[a, cells - 1, 1:2, :])
+        product = -(block[a, cells - 1] * rates[a, cells - 1, 1:2, :])
         for c in reversed(range(cells - 1)):
             turned = answers[c] - apply(outer, (a, c), turned)
             product = -apply(outer, (a, c), product)
-        return turned, product
+        target[0, i] = answers[-1]
+        target[1, i] = turned
+        target[2, i] = product
 
     def first_guess(source, a):
         previous = apply(plain, (a, 0), source[a, 0])
@@ -214,15 +220,14 @@
     def ordered(own, foreign):
         return jnp.where(is_first, own, foreign), jnp.where(is_first, foreign, own)
 
-    for i in range(half):
-        forms(other[i])
-    kept = [inner_responses(other[i]) for i in range(half)]
-    for i in range(half):
-        sent_matrix[0, i] = kept[i][-1]
     peers = 1 + sum(jnp.where(exists, 1, 0) for exists, device in neighbours)
     pl.semaphore_wait(barrier, peers)
     for i in range(half):
-        swap_matrix(0, i).start()
+        swap_radial(i).start()
+        for c in range(cells):
+            swap_block(i, c).start()
+    for i in range(half):
+        forms(other[i])
 
     for sweep in range(SWEEPS):
         if sweep == 0:
@@ -259,25 +264,20 @@
             swap(sweep, 1, i).start()
         if sweep == 0:
             for i in range(half):
-                turned, product = other_responses(other[i], kept[i])
-                sent_matrix[1, i] = turned
-                swap_matrix(1, i).start()
-                sent_matrix[2, i] = product
-                swap_matrix(2, i).start()
-            for i in range(half):
-                a = mine[i]
-                forms(a)
-                answers = inner_responses(a)
-                turned, product = other_responses(a, answers)
-                own_matrix[0, i] = answers[-1]
-                own_matrix[1, i] = turned
-                own_matrix[2, i] = product
+                forms(mine[i])
+                responses(own_matrix, i, inverse, radial, inner, outer, mine[i])
         for i in range(half):
             local[0, i] = first_guess(source, mine[i])
             local[1, i] = first_turn(mine[i])
         if sweep == 0:
             for i in range(half):
-                swap_matrix(0, i).wait_recv()
+                swap_radial(i).wait_recv()
+                for c in range(cells):
+                    swap_block(i, c).wait_recv()
+                    block = got_block[i, c]
+                    keep(far_inner, (i, c), block * got_radial[i, c, 0:1, :])
+                    keep(far_outer, (i, c), block * got_radial[i, c, 1:2, :])
+                responses(got_matrix, i, got_block, got_radial, far_inner, far_outer, i)
                 near, far = ordered(own_matrix[0, i], got_matrix[0, i])
                 keep(pair, (0, i), near)
                 keep(pair, (1, i), far)
@@ -285,8 +285,6 @@
         up, down = 2 * sweep, 2 * sweep + 1
 
         def late_forms(i):
-            swap_matrix(1, i).wait_recv()
-            swap_matrix(2, i).wait_recv()
             near, far = ordered(own_matrix[1, i], got_matrix[1, i])
             keep(pair, (3, i), near)
             keep(pair, (4, i), far)
@@ -440,8 +438,9 @@
                 share(other[i])
 
     for i in range(half):
-        for kind in range(3):
-            swap_matrix(kind, i).wait_send()
+        swap_radial(i).wait_send()
+        for c in range(cells):
+            swap_block(i, c).wait_send()
         for sweep in range(SWEEPS):
             for kind in range(4):
                 swap(sweep, kind, i).wait_send()
@@ -476,6 +475,7 @@
     assert segments % 2 == 0 and segments >= 6 and stations == WIDTH
     axial = axial_coupling.reshape(-1, species).T
     matrix = pltpu.VMEM((stations, cells, 2, species, species), jnp.bfloat16)
+    far_matrix = pltpu.VMEM((half, cells, 2, species, species), jnp.bfloat16)
     square = pltpu.VMEM((3, half, species, species), jnp.float32)
     grid = pltpu.VMEM((stations, cells, species, columns), jnp.float32)
     swaps = pltpu.VMEM((SWEEPS, 4, half, species, columns), jnp.float32)
@@ -484,7 +484,7 @@
     fold = pltpu.VMEM((half, species, species), jnp.float32)
     sems = [
         pltpu.SemaphoreType.DMA(shape)
-        for shape in ((3, half), (SWEEPS, 4, half), (2 * SWEEPS, half), (2, stations), (SWEEPS, half), (half,))
+        for shape in ((cells + 1, half), (SWEEPS, 4, half), (2 * SWEEPS, half), (2, stations), (SWEEPS, half), (half,))
         for side in range(2)
     ]
     spec = pl.BlockSpec(memory_space=pltpu.VMEM)
@@ -498,7 +498,10 @@
             matrix,
             matrix,
             pltpu.VMEM((10, half, 2, species, species), jnp.bfloat16),
-            square,
+            far_matrix,
+            far_matrix,
+            pltpu.VMEM((half, cells, species, species), jnp.float32),
+            pltpu.VMEM((half, *radial_coupling.shape[1:]), jnp.float32),
             square,
             square,
             fold,

time: 76.4 us -> 71.7 us (0.938)
  Pallas kernels: 71.4 us -> 67.1 us
    pallas_call x1, Pallas kernels: 71.4 us -> 67.1 us  [on_device(): pl.pallas_call(functools.partial(kernel, segments, blocks), out_shape=jax...]
where the time goes in v4:
time: 71.7 us; the launch traced here: 71.4 us
  Pallas kernels  67.1 us (94%)
  local copies, waits for them, and re-layouts  4.32 us (6%)
    pallas_call x1, Pallas kernels, on_device(): pl.pallas_call(functools.partial(kernel, segments, blocks), out_shape=jax...  67.1 us
    unnamed x7, local copies, waits for them, and re-layouts  3.5 us

profile of v4, /device:TPU:0, one launch (start us, length us, event | category | flops | bytes accessed | tf_op | source)
XLA Modules:
  0.0 71.4 jit_solution(4914417599011002519)
XLA Ops:
  0.0 0.7 %reshape.3 = f32[16,200]{1,0:T(8,128)S(1)} reshape(f32[2,2,4,200]{3,2,1,0:T(4,128)} %param.7) | data formatting | bytes 25600 | tf_op jit(solution)/shard_map/reshape | solution.py:476
  0.7 0.0 copy-start.2
  0.7 0.1 copy.6
  0.8 0.6 copy-done.2
  1.4 0.0 copy-start
  1.4 1.1 %copy-done = f32[2,2,200,200]{3,2,1,0:T(8,128)S(1)} copy-done((f32[2,2,200,200]{3,2,1,0:T(8,128)S(1)}, f32[2,2,200,200]{3,2,1,0:T(8,128)}, u32[]{:S(2)}) %copy-start) | copy-done | bytes 640024
  2.6 0.0 copy-start.1
  2.6 1.0 %copy-done.1 = f32[2,2,200,128]{3,2,1,0:T(8,128)S(1)} copy-done((f32[2,2,200,128]{3,2,1,0:T(8,128)S(1)}, f32[2,2,200,128]{3,2,1,0:T(8,128)}, u32[]{:S(2)}) %copy-start.1) | copy-done | bytes 409624
  3.6 67.1 %shard_map.46 = f32[2,2,200,128]{3,2,1,0:T(8,128)S(1)} custom-call(f32[2,2,200,128]{3,2,1,0:T(8,128)S(1)} %copy-done.1, f32[2,2,200,200]{3,2,1,0:T(8,128)S(1)} %copy-done, f32[2,2,2,200]{3,2,1,0:T(2,128)S(1)} %copy-done.2, f32[200,16]{1,0:T(8,128)S(1)} %bitcast.1), custom_call_target="tpu_custom_call" | custom-call | tf_op jit(solution)/shard_map/pallas_call | solution.py:491
  70.6 0.8 %copy.8 = f32[2,2,200,128]{3,2,1,0:T(8,128)} copy(f32[2,2,200,128]{3,2,1,0:T(8,128)S(1)} %shard_map.46) | data formatting | bytes 819200
Async XLA Ops:
  0.7 0.7 copy-start.2
  1.4 1.1 %copy-start = (f32[2,2,200,200]{3,2,1,0:T(8,128)S(1)}, f32[2,2,200,200]{3,2,1,0:T(8,128)}, u32[]{:S(2)}) copy-start(f32[2,2,200,200]{3,2,1,0:T(8,128)} %inverse.1) | copy-start | bytes 1920004
  2.6 1.0 %copy-start.1 = (f32[2,2,200,128]{3,2,1,0:T(8,128)S(1)}, f32[2,2,200,128]{3,2,1,0:T(8,128)}, u32[]{:S(2)}) copy-start(f32[2,2,200,128]{3,2,1,0:T(8,128)} %sources.1) | copy-start | bytes 1228804

commit v5 on v4

--- a/solution.py
+++ b/solution.py
@@ -34,11 +34,13 @@
 def kernel(
     segments,
     blocks,
-    sources,
-    inverse,
+    given_sources,
+    given_inverse,
     radial,
     axial,
     out,
+    sources,
+    inverse,
     plain,
     inner,
     outer,
@@ -75,7 +77,14 @@
     early_recv,
     fold_send,
     fold_recv,
+    load_sem,
 ):
+    loads = (
+        pltpu.make_async_copy(given_inverse, inverse, load_sem.at[0]),
+        pltpu.make_async_copy(given_sources, sources, load_sem.at[1]),
+    )
+    for load in loads:
+        load.start()
     stations, cells = sources.shape[:2]
     half = stations // 2
     rad = lax.axis_index("rad")
@@ -117,7 +126,7 @@
 
     def swap_block(i, c):
         at = (c, i)
-        source = inverse.at[other[i], c]
+        source = given_inverse.at[other[i], c]
         return remote(source, got_block.at[i, c], matrix_send.at[at], matrix_recv.at[at], partner)
 
     def swap_radial(i):
@@ -226,6 +235,8 @@
         swap_radial(i).start()
         for c in range(cells):
             swap_block(i, c).start()
+    for load in loads:
+        load.wait()
     for i in range(half):
         forms(other[i])
 
@@ -488,12 +499,16 @@
         for side in range(2)
     ]
     spec = pl.BlockSpec(memory_space=pltpu.VMEM)
+    raw = pl.BlockSpec(memory_space=pl.ANY)
+    sems.append(pltpu.SemaphoreType.DMA((2,)))
     return pl.pallas_call(
         functools.partial(kernel, segments, blocks),
         out_shape=jax.ShapeDtypeStruct(sources.shape, jnp.float32),
-        in_specs=[spec] * 4,
+        in_specs=[raw, raw, spec, spec],
         out_specs=spec,
         scratch_shapes=[
+            grid,
+            pltpu.VMEM(block_inverse.shape, jnp.float32),
             matrix,
             matrix,
             matrix,
@@ -521,7 +536,7 @@
             *sems,
         ],
         compiler_params=pltpu.CompilerParams(
-            collective_id=0, has_side_effects=True, vmem_limit_bytes=48 << 20
+            collective_id=0, has_side_effects=True, vmem_limit_bytes=63 << 20
         ),
     )(sources, block_inverse, radial_coupling, axial)
 

time: 71.7 us -> 72.6 us (1.013)
  Pallas kernels: 67.1 us -> 69.1 us
  local copies, waits for them, and re-layouts: 4.32 us -> 3.25 us
    pallas_call x1, Pallas kernels: 67.1 us -> 69.1 us  [on_device(): pl.pallas_call(functools.partial(kernel, segments, blocks), out_shape=jax...]
    unnamed x7 -> x1, local copies, waits for them, and re-layouts: 3.5 us -> 1.78 us
where the time goes in v5:
time: 72.6 us; the launch traced here: 72.3 us
  Pallas kernels  69.1 us (95%)
  local copies, waits for them, and re-layouts  3.25 us (4%)
    pallas_call x1, Pallas kernels, on_device(): pl.pallas_call(functools.partial(kernel, segments, blocks), out_shape=jax...  69.1 us
    unnamed x1, local copies, waits for them, and re-layouts  1.78 us
    reshape x2, local copies, waits for them, and re-layouts, on_device(): axial = axial_coupling.reshape(-1, species).T  1.47 us

profile of v5, /device:TPU:0, one launch (start us, length us, event | category | flops | bytes accessed | tf_op | source)
XLA Modules:
  0.0 72.3 jit_solution(18426254341813916887)
XLA Ops:
  0.0 0.7 %reshape.3 = f32[16,200]{1,0:T(8,128)S(1)} reshape(f32[2,2,4,200]{3,2,1,0:T(4,128)} %param.7) | data formatting | bytes 25600 | tf_op jit(solution)/shard_map/reshape | solution.py:487
  0.7 0.7 %copy.6 = f32[16,200]{0,1:T(8,128)} copy(f32[16,200]{1,0:T(8,128)S(1)} %reshape.3) | data formatting | bytes 25600 | tf_op jit(solution)/shard_map/reshape | solution.py:487
  1.5 69.1 %shard_map.46 = f32[2,2,200,128]{3,2,1,0:T(8,128)} custom-call(f32[2,2,200,128]{3,2,1,0:T(8,128)} %given_sources.1, f32[2,2,200,200]{3,2,1,0:T(8,128)} %given_inverse.1, f32[2,2,2,200]{3,2,1,0:T(2,128)} %radial.1, f32[200,16]{1,0:T(8,128)} %bitcast.1), custom_call_target="tpu_custom_call" | custom-call | tf_op jit(solution)/shard_map/pallas_call | solution.py:504
  70.5 1.8 %copy.8 = f32[2,2,200,128]{3,2,1,0:T(8,128)} copy(f32[2,2,200,128]{3,2,1,0:T(8,128)} %shard_map.46) | data formatting | bytes 819200
